TPU v7x, 512 devices: a whole 4x4x16 slice. The times are simulated.
512 devices in a mesh: rows: 64 (over y, z_lo, core), feat: 8 (over x, z_hi).
Axes of the slice: x: 4, y: 4, z: 16 (z_hi: 2, z_lo: 8; z = z_hi * 8 + z_lo), core: 2. Of those that a mesh axis runs over, the one named last changes fastest.
Arguments:
- logits: float32 [196608, 32], P('rows'), may hold values from -6 to 6
- labels: int32 [196608], P('rows'), may hold values from 0 to 31
- node_ids: int32 [196608], P('rows'), may hold values from 0 to 7
- bin_codes: int32 [196608, 256], P('rows', 'feat'), may hold values from 0 to 63
- split_feature: int32 [8], replicated, may hold values from 0 to 255
- split_bin: int32 [8], replicated, may hold values from 1 to 63
- split_missing: int32 [8], replicated, may hold values from 0 to 1
Outputs:
- new_logits: float32 [196608, 32], P('rows')
- gain_table: float32 [64, 32, 128], P('rows', 'feat')
- leaves: float32 [8, 2, 32], replicated
Inputs may be any that keep to these rules, and one draw needn't show every extreme that they name: `split_missing`: 1 sends the missing code 64 - 1 to the left child, 0 to the right child.
All inputs are finite; a program needn't handle non-finite values.
Results may differ from a plain program's by a relative error of at most 0.0014.
Values sent between devices are 32-bit elements; how exact they have to be, the bound alone decides.
A program may use at most 64 MiB of HBM per device.

v0:
```python
import math

import jax
import jax.numpy as jnp
from jax import lax
from jax.sharding import PartitionSpec as P

BINS = 64


reg_lambda = 1.0
step_size = 0.3


def split_score(sums, classes):
    grad_part = sums[..., :classes]
    hess_part = sums[..., classes:]
    return jnp.sum(grad_part * grad_part / (hess_part + reg_lambda), axis=-1)


def local(logits, labels, node_ids, bin_codes, split_feature, split_bin, split_missing):
    rows_dev, classes = logits.shape
    feats_dev = bin_codes.shape[1]
    node_count = split_feature.shape[0]
    bin_count = BINS
    per_node = lax.axis_size("rows") // node_count
    pairs_dev = feats_dev // per_node
    feat_pairs = feats_dev // 2
    width = 2 * classes
    expo_vals = jnp.exp(logits)
    soft_prob = expo_vals / jnp.sum(expo_vals, axis=1, keepdims=True)
    class_iota = jnp.arange(classes, dtype=jnp.int32)
    target = (labels[:, None] == class_iota[None, :]).astype(jnp.float32)
    grad_hess = jnp.concatenate(
        [
            (soft_prob - target).astype(jnp.bfloat16),
            (soft_prob * (1.0 - soft_prob)).astype(jnp.bfloat16),
        ],
        axis=1,
    )
    node_iota = jnp.arange(node_count, dtype=jnp.int32)
    node_match = node_ids[:, None] == node_iota[None, :]
    masked_rows = jnp.where(
        node_match[:, :, None], grad_hess[:, None, :], jnp.zeros((), jnp.bfloat16)
    ).reshape(rows_dev, node_count * width)
    bin_iota = jnp.arange(bin_count, dtype=jnp.int32)
    feat_block = math.gcd(feats_dev, 8)
    block_count = feats_dev // feat_block

    def make_hot(codes):
        return (
            (codes[:, :, None] == bin_iota[None, None, :])
            .astype(jnp.bfloat16)
            .reshape(rows_dev, codes.shape[1] * bin_count)
        )

    own_rows = node_count * feat_pairs * width // lax.axis_size("rows")
    groups = lax.axis_size("rows") * own_rows // width
    node_span = groups // feat_pairs

    def block_product(block):
        block_codes = lax.dynamic_slice_in_dim(bin_codes, block * feat_block, feat_block, 1)
        return lax.dot_general(
            masked_rows,
            make_hot(block_codes),
            (((0,), (0,)), ((), ())),
            preferred_element_type=jnp.float32,
        )

    stacked = lax.map(block_product, jnp.arange(block_count, dtype=jnp.int32))
    product = stacked.transpose(1, 0, 2).reshape(node_span * width, feats_dev * bin_count)
    product = product.reshape(node_span, width, feat_pairs, 2 * bin_count).transpose(0, 2, 1, 3)
    owned_hist = lax.psum_scatter(
        product.reshape(lax.axis_size("rows") * own_rows, 2 * bin_count),
        "rows",
        scatter_dimension=0,
        tiled=True,
    )
    owned = (
        owned_hist.reshape(pairs_dev // 2, width, 2, bin_count)
        .transpose(0, 2, 3, 1)
        .reshape(pairs_dev, bin_count, width)
    )
    lower_mask = (
        (bin_iota[:, None] < bin_iota[None, :]) & (bin_iota[:, None] < bin_count - 1)
    ).astype(jnp.float32)
    left_base = jnp.einsum("pbc,bt->ptc", owned, lower_mask, precision=lax.Precision.HIGHEST)
    node_total = jnp.sum(owned, axis=1, keepdims=True)
    missing_sum = owned[:, bin_count - 1 :, :]
    left_miss = left_base + missing_sum
    parent_score = split_score(node_total, classes)
    gain_left = (
        split_score(left_miss, classes)
        + split_score(node_total - left_miss, classes)
        - parent_score
    )
    gain_right = (
        split_score(left_base, classes)
        + split_score(node_total - left_base, classes)
        - parent_score
    )
    gain_rows = (jnp.concatenate([gain_left, gain_right], axis=1) / (2.0 * classes))[None]
    row_feature = jnp.sum(jnp.where(node_match, split_feature[None, :], 0), axis=1)
    row_bin = jnp.sum(jnp.where(node_match, split_bin[None, :], 0), axis=1)
    row_missing = jnp.sum(jnp.where(node_match, split_missing[None, :], 0), axis=1)
    feat_index = lax.axis_index("feat")
    local_col = row_feature - feat_index * feats_dev
    is_owned = (local_col >= 0) & (local_col < feats_dev)
    col_iota = jnp.arange(feats_dev, dtype=jnp.int32)
    row_code = jnp.sum(jnp.where(col_iota[None, :] == local_col[:, None], bin_codes, 0), axis=1)
    goes_left = (row_code < row_bin) | (row_code == bin_count - 1) & (row_missing == 1)
    right_flag = jnp.where(is_owned & jnp.logical_not(goes_left), 1.0, 0.0).astype(jnp.float32)
    side_count = lax.psum(right_flag, "feat")
    row_side = (side_count > 0.5).astype(jnp.int32)
    slot_iota = jnp.arange(2 * node_count, dtype=jnp.int32)
    slot_hot = (node_ids * 2 + row_side)[:, None] == slot_iota[None, :]
    row_index = lax.axis_index("rows")
    my_node = row_index // per_node
    base_feat = feat_index * feats_dev + row_index % per_node * pairs_dev
    local_feat = split_feature[my_node] - base_feat
    holds = ((local_feat >= 0) & (local_feat < pairs_dev)).astype(jnp.float32)
    chosen = owned[jnp.clip(local_feat, 0, pairs_dev - 1)]
    bin_mask = ((bin_iota < split_bin[my_node]) & (bin_iota < bin_count - 1)).astype(jnp.float32)
    left_sum = jnp.sum(chosen * bin_mask[:, None], axis=0) + chosen[bin_count - 1] * split_missing[
        my_node
    ].astype(jnp.float32)
    node_sum = jnp.sum(chosen, axis=0)
    entry = jnp.stack([left_sum, node_sum - left_sum], axis=0) * holds
    placed = jnp.where(
        (node_iota == my_node)[:, None, None], entry[None], jnp.zeros((), jnp.float32)
    )
    side_sums = lax.psum(placed, ("rows", "feat"))
    leaves = -side_sums[..., :classes] / (side_sums[..., classes:] + reg_lambda)
    update = jnp.dot(
        slot_hot.astype(jnp.float32),
        leaves.reshape(2 * node_count, classes),
        precision=lax.Precision.HIGHEST,
    )
    new_logits = logits + step_size * update
    return (new_logits, gain_rows, leaves)


def solution(mesh):
    return jax.shard_map(
        local,
        mesh=mesh,
        in_specs=(P("rows", None), P("rows"), P("rows"), P("rows", "feat"), P(), P(), P()),
        out_specs=(P("rows", None), P("rows", "feat", None), P()),
        check_vma=False,
    )
```

profile of v0, /device:TPU:1, one launch (start us, length us, event | category | flops | bytes accessed | tf_op | source)
XLA Modules:
  0.0 613.6 jit_solution(12515425515692365684)
XLA Ops:
  7.2 1.1 exponential_reduce_fusion
  8.3 0.7 iota_compare_fusion.4
  9.0 1.1 subtract_convert_fusion
  10.2 25.2 %while.11 = (s32[]{:T(128)}, f32[4,512,512]{1,2,0:T(8,128)}, s32[4]{0:T(128)S(1)}, s32[3072,32]{0,1:T(8,128)}, bf16[3072,64]{0,1:T(8,128)(2,1)S(1)}, /*index=5*/...) while((s32[]{:T(128)}, f32[4,512,512]{1,2,0:T(8,128)}, ...), condition=%wide.region_7.8_spmd.clone, body=%wide.region_6.7_spmd.clone.sunk | while | flops 1613758464 | bytes 11207331 | solution.py:70
  10.2 0.6 dynamic_slice.31
  11.5 0.9 constant_dynamic-slice_fusion.2
  12.4 0.1 eq.180
  12.4 0.9 bitcast_compare_fusion.2
  13.4 0.3 broadcast_select_fusion.3
  13.7 2.8 fusion.35
  16.5 0.6 dynamic_slice.31
  17.7 0.9 constant_dynamic-slice_fusion.2
  18.7 0.9 bitcast_compare_fusion.2
  19.6 0.3 broadcast_select_fusion.3
  19.9 2.8 fusion.35
  22.8 0.6 dynamic_slice.31
  24.0 0.9 constant_dynamic-slice_fusion.2
  25.0 0.9 bitcast_compare_fusion.2
  26.0 0.3 broadcast_select_fusion.3
  26.3 2.8 fusion.35
  29.1 0.6 dynamic_slice.31
  30.3 0.9 constant_dynamic-slice_fusion.2
  31.2 0.1 eq.180
  31.3 0.9 bitcast_compare_fusion.2
  32.2 0.3 broadcast_select_fusion.3
  32.5 2.8 fusion.35
  35.4 5.4 copy.31
  40.8 5.5 reshape_reshape.3
  46.3 5.4 copy.32
  51.7 0.6 copy-done.4
  52.3 0.6 dynamic_slice.19
  53.5 0.6 dynamic_slice.21
  54.1 0.6 dynamic_slice.22
  55.4 0.2 select_reduce_fusion.2
  55.6 75.7 %psum.14 = f32[3072]{0:T(1024)S(1)} all-reduce(f32[3072]{0:T(1024)S(1)} %and_select_fusion), channel_id=1, replica_groups=mesh['rows'=64,'feat'=8] {'feat'}, use_global_device_ids=true, to_apply=%region_4.5 | all-reduce | flops 3072 | bytes 24576 | tf_op jit(solution)/shard_map/psum | solution.py:113
  131.4 0.7 and_convert_fusion
  132.1 359.6 %reduce-scatter.2.cloned.1.call-done = f32[128,128]{1,0:T(8,128)} async-done(((f32[8192,128]{1,0:T(8,128)}), f32[128,128]{1,0:T(8,128)}) %reduce-scatter.2.cloned.1.call-update) | async-done | bytes 65552 | tf_op jit(solution)/shard_map/reduce_scatter | solution.py:73
  491.6 1.0 reshape.173
  492.6 0.1 copy.33
  492.7 0.2 bitcast_reduce_fusion
  493.0 0.1 copy.35
  493.1 0.2 fusion.22
  493.3 0.1 fusion.16
  493.5 110.9 %psum.15 = f32[8,2,64]{2,1,0:T(2,128)S(1)} all-reduce(f32[8,2,64]{2,1,0:T(2,128)S(1)} %broadcast_select_fusion.1), channel_id=1, replica_groups=mesh['rows'=64,'feat'=8] {'rows','feat'}, use_global_device_ids=true, to_apply=%region_11.12 | all-reduce | flops 1024 | bytes 8192 | tf_op jit(solution)/shard_map/psum | solution.py:132
  604.4 0.1 fusion.21
  604.5 0.3 broadcast_subtract_fusion.1
  605.0 0.7 maximum_multiply_fusion
  605.6 1.1 fusion.5
  (39 shorter events, 0.7 us)
Async XLA Ops:
  7.2 484.5 %reduce-scatter.2.cloned.1.call-start = ((), (), s32[]{:S(2)}) async-start(), calls=%async_computation.1 | async-start | bytes 4259840 | tf_op jit(solution)/shard_map/reduce_scatter | solution.py:73
  51.6 0.7 copy-start.4
  51.6 1.9 copy-start.6
  51.6 2.5 copy-start.5
  51.6 3.7 copy-start.2
  51.6 3.9 copy-start.1
  51.6 554.0 %copy-start = (f32[3072,32]{0,1:T(8,128)S(1)}, f32[3072,32]{0,1:T(8,128)}, u32[]{:S(2)}) copy-start(f32[3072,32]{0,1:T(8,128)} %param.9) | copy-start | bytes 1179652
  604.5 2.2 copy-start.3
Sparse Core Ops, SparseCore 0:
  51.8 439.8 reduce-scatter.1
where the time goes:
time: 614 us
  waiting for transfers between devices  360 us (59%)
  blocking collectives  187 us (30%)
  local copies, waits for them, and re-layouts  26 us (4%)
  between operations  15.6 us (3%)
  matrix products  12.7 us (2%)
  other arithmetic  10.3 us (2%)
    reduce_scatter x1, waiting for transfers between devices, local(): lax.psum_scatter(product.reshape(lax.axis_size('rows') * own_rows, 2 * bi...  360 us
    psum x1, blocking collectives, local(): side_sums = lax.psum(placed, ('rows', 'feat'))  111 us
    psum x1, blocking collectives, local(): side_count = lax.psum(right_flag, 'feat')  75.7 us
  transfers between devices with their start and end apart: 1, of which 1 were waited for; matrix products, arithmetic and copies ran while one was open for 0% of the time, Pallas kernels for 0%

commit v1 on v0

v1 whole, which is shorter than its diff:
```python
import jax
import jax.numpy as jnp
from jax import lax
from jax.experimental import pallas as pl
from jax.experimental.pallas import tpu as pltpu
from jax.sharding import PartitionSpec as P

BINS = 64
MESH = pl.DeviceIdType.MESH
reg_lambda = 1.0
step_size = 0.3
LANE_BLOCK = 512
NT = (((1,), (1,)), ((), ()))
NN = (((1,), (0,)), ((), ()))


def split3(x):
    hi = x.astype(jnp.bfloat16)
    rest = x - hi.astype(jnp.float32)
    mid = rest.astype(jnp.bfloat16)
    low = (rest - mid.astype(jnp.float32)).astype(jnp.bfloat16)
    return hi, mid, low


def exact_dot(x, weights, dims):
    hi, mid, low = split3(x)
    dot = lambda part: lax.dot_general(part, weights, dims, preferred_element_type=jnp.float32)
    return dot(hi) + (dot(mid) + dot(low))


def ratio(sums):
    grad_part = sums[:32]
    hess_part = sums[32:]
    return jnp.sum(grad_part * grad_part / (hess_part + reg_lambda), axis=0, keepdims=True)


def kernel(
    feature_ref,
    bin_ref,
    missing_ref,
    logits_ref,
    labels_ref,
    nodes_ref,
    codes_ref,
    new_ref,
    gain_ref,
    leaves_ref,
    masked,
    hot,
    hist,
    core_buf,
    y1_buf,
    y2_buf,
    z1_buf,
    z2_buf,
    z3_buf,
    flag_buf,
    s1_buf,
    s2_buf,
    s3_buf,
    core_send,
    core_recv,
    y1_send,
    y1_recv,
    y2_send,
    y2_recv,
    z1_send,
    z1_recv,
    z2_send,
    z2_recv,
    z3_send,
    z3_recv,
    flag_send,
    flag_recv,
    s1_send,
    s1_recv,
    s2_send,
    s2_recv,
    s3_send,
    s3_recv,
):
    rows = logits_ref.shape[1]
    row = lax.axis_index("rows")
    feat = lax.axis_index("feat")
    core = row % 2
    z = (row // 2) % 8
    y = row // 16
    z0, z1, z2 = z % 2, (z // 2) % 2, z // 4
    group = y * 2 + core
    ya = y + 1 - 2 * (y % 2)
    yb = 3 - y
    yc = 3 - ya

    def at_y(other):
        return other * 16 + z * 2 + core

    core_peer = row + 1 - 2 * core
    z_peer1 = row + 2 * (1 - 2 * z0)
    z_peer2 = row + 4 * (1 - 2 * z1)
    z_peer4 = row + 8 * (1 - 2 * z2)

    def feat_peer(d):
        return (row, (feat + d) % 8)

    def group_peer(d):
        other = (group + d) % 8
        return ((other // 2) * 16 + z * 2 + other % 2, feat)

    def z_peer(d):
        return (y * 16 + ((z + d) % 8) * 2 + core, feat)

    barrier = pltpu.get_barrier_semaphore()
    for d in range(1, 8):
        for peer in (feat_peer(d), group_peer(d), z_peer(d)):
            pl.semaphore_signal(barrier, inc=1, device_id=peer, device_id_type=MESH)

    iota16 = lax.broadcasted_iota(jnp.int32, (16, LANE_BLOCK), 0)
    iota32 = lax.broadcasted_iota(jnp.int32, (32, LANE_BLOCK), 0)
    one, zero = jnp.float32(1.0), jnp.float32(0.0)

    def prepare(i, side_sums):
        at = pl.ds(pl.multiple_of(i * LANE_BLOCK, LANE_BLOCK), LANE_BLOCK)
        expo = jnp.exp(logits_ref[:, at])
        prob = expo / jnp.sum(expo, axis=0, keepdims=True)
        target = jnp.where(iota32 == labels_ref[:, at], one, zero)
        grad = (prob - target).astype(jnp.bfloat16).astype(jnp.float32)
        hess = (prob * (1.0 - prob)).astype(jnp.bfloat16).astype(jnp.float32)
        both = jnp.concatenate([grad, hess], axis=0)
        node = nodes_ref[:, at]
        row_feature = jnp.zeros_like(node)
        row_bin = jnp.zeros_like(node)
        row_missing = jnp.zeros_like(node)
        for n in range(8):
            here = node == n
            masked[n * 64 : (n + 1) * 64, at] = jnp.where(here, both, zero).astype(jnp.bfloat16)
            row_feature = jnp.where(here, feature_ref[n], row_feature)
            row_bin = jnp.where(here, bin_ref[n], row_bin)
            row_missing = jnp.where(here, missing_ref[n], row_missing)
        column = row_feature - feat * 32
        owned = (column >= 0) & (column < 32)
        code = jnp.sum(
            jnp.where(iota32 == column, codes_ref[:, at].astype(jnp.float32), zero),
            axis=0,
            keepdims=True,
        ).astype(jnp.int32)
        left = (code < row_bin) | ((code == BINS - 1) & (row_missing == 1))
        right = jnp.where(left, 0, 1)
        flag_buf[feat, :, at] = jnp.where(owned, right, 0).astype(jnp.float32)
        slot = jnp.where(owned, node * 2 + right, -1)
        slot_hot = jnp.where(iota16 == slot, one, zero).astype(jnp.bfloat16)
        return side_sums + lax.dot_general(
            slot_hot, both.astype(jnp.bfloat16), NT, preferred_element_type=jnp.float32
        )

    side_sums = lax.fori_loop(
        0, rows // LANE_BLOCK, prepare, jnp.zeros((16, 64), jnp.float32)
    )
    s1_buf[feat] = jnp.concatenate([side_sums, jnp.zeros((16, 64), jnp.float32)], axis=1)

    pl.semaphore_wait(barrier, 21)

    def exchange(buf, send, recv, mine, peer):
        def copy(d, slot):
            return pltpu.make_async_remote_copy(
                src_ref=buf.at[slot],
                dst_ref=buf.at[slot],
                send_sem=send.at[d - 1],
                recv_sem=recv.at[slot],
                device_id=peer(d),
                device_id_type=MESH,
            )

        def start():
            for d in range(1, 8):
                copy(d, mine).start()

        def arrive():
            for d in range(1, 8):
                copy(d, (mine + d) % 8).wait_recv()

        def finish():
            for d in range(1, 8):
                copy(d, mine).wait_send()

        return start, arrive, finish

    flags = exchange(flag_buf, flag_send, flag_recv, feat, feat_peer)
    stage1 = exchange(s1_buf, s1_send, s1_recv, feat, feat_peer)
    stage2 = exchange(s2_buf, s2_send, s2_recv, group, group_peer)
    stage3 = exchange(s3_buf, s3_send, s3_recv, z, z_peer)
    stage1[0]()
    flags[0]()

    def total(buf):
        sums = buf[0]
        for i in range(1, 8):
            sums = sums + buf[i]
        return sums

    def remote(src, dst, send, recv, peer):
        return pltpu.make_async_remote_copy(
            src_ref=src,
            dst_ref=dst,
            send_sem=send,
            recv_sem=recv,
            device_id=(peer, feat),
            device_id_type=MESH,
        )

    def core_copy(k):
        return remote(
            hist.at[2 * k], core_buf.at[k], core_send.at[k], core_recv.at[k], core_peer
        )

    def first_y(k):
        colour = k % 2
        return ya + colour * (yb - ya)

    def second_y(k):
        colour = k % 2
        return yb + colour * (ya - yb)

    def y1_copy(k, part):
        dest = first_y(k) if part else yc
        return remote(
            hist.at[2 * k + 1, :, pl.ds(2 * dest, 2)],
            y1_buf.at[k, part],
            y1_send.at[k, part],
            y1_recv.at[k, part],
            at_y(first_y(k)),
        )

    def y2_copy(k):
        dest = second_y(k)
        return remote(
            hist.at[2 * k + 1, :, pl.ds(2 * dest, 2)],
            y2_buf.at[k],
            y2_send.at[k],
            y2_recv.at[k],
            at_y(dest),
        )

    mine_y = pl.ds(2 * y, 2)

    def z1_copy(colour):
        k = 2 * (1 - z0) + colour
        return remote(
            hist.at[2 * k + 1, :, mine_y],
            z1_buf.at[colour],
            z1_send.at[colour],
            z1_recv.at[colour],
            z_peer1,
        )

    def z2_copy(colour):
        k = 2 * z0 + colour
        return remote(
            hist.at[2 * k + 1, 1 - z1, mine_y],
            z2_buf.at[colour],
            z2_send.at[colour],
            z2_recv.at[colour],
            z_peer2,
        )

    def z3_copy(colour):
        k = 2 * z0 + colour
        return remote(
            hist.at[2 * k + 1, z1, 2 * y + 1 - z2],
            z3_buf.at[colour],
            z3_send.at[colour],
            z3_recv.at[colour],
            z_peer4,
        )

    iota64 = lax.broadcasted_iota(jnp.int32, (64, rows), 0)

    def after_core(k):
        core_copy(k).wait_recv()
        hist[2 * k + 1] = hist[2 * k + 1] + core_buf[k]
        y1_copy(k, 0).start()
        y1_copy(k, 1).start()

    def step(s, carry):
        k = s // 2
        side = s % 2
        half, colour = k // 2, k % 2
        owner = side * core + (1 - side) * (1 - core)
        base = half * 8 + owner * 4 + colour * 2
        for high in range(2):
            for low in range(2):
                code = codes_ref[pl.ds(base + 16 * high + low, 1), :]
                start = (high * 2 + low) * 64
                hot[start : start + 64, :] = jnp.where(code == iota64, one, zero).astype(
                    jnp.bfloat16
                )
        out = lax.dot_general(masked[...], hot[...], NT, preferred_element_type=jnp.float32)
        for high in range(2):
            for n in range(8):
                hist[s, high, n] = out[n * 64 : (n + 1) * 64, high * 128 : (high + 1) * 128]

        @pl.when(side == 0)
        def _():
            core_copy(k).start()

        @pl.when((side == 0) & (k > 0))
        def _():
            after_core(k - 1)

        return carry

    lax.fori_loop(0, 8, step, 0)
    after_core(3)

    def after_y1(k):
        y1_copy(k, 0).wait_recv()
        at = pl.ds(2 * second_y(k), 2)
        hist[2 * k + 1, :, at] = hist[2 * k + 1, :, at] + y1_buf[k, 0]
        y2_copy(k).start()
        y1_copy(k, 1).wait_recv()
        hist[2 * k + 1, :, mine_y] = hist[2 * k + 1, :, mine_y] + y1_buf[k, 1]

    def after_y2(k):
        y2_copy(k).wait_recv()
        hist[2 * k + 1, :, mine_y] = hist[2 * k + 1, :, mine_y] + y2_buf[k]

        @pl.when(z0 != k // 2)
        def _():
            z1_copy(k % 2).start()

    def after_z1(colour):
        z1_copy(colour).wait_recv()
        k = 2 * z0 + colour
        hist[2 * k + 1, :, mine_y] = hist[2 * k + 1, :, mine_y] + z1_buf[colour]
        z2_copy(colour).start()

    def after_z2(colour):
        z2_copy(colour).wait_recv()
        k = 2 * z0 + colour
        hist[2 * k + 1, z1, mine_y] = hist[2 * k + 1, z1, mine_y] + z2_buf[colour]
        z3_copy(colour).start()

    stage1[1]()
    s2_buf[group] = total(s1_buf)
    stage2[0]()
    after_y1(0)
    after_y1(1)
    stage2[1]()
    s3_buf[z] = total(s2_buf)
    stage3[0]()
    after_y2(0)
    after_y2(1)
    after_y1(2)
    after_y1(3)

    stage3[1]()
    flags[1]()
    sums = total(s3_buf)
    sums_t = jnp.transpose(sums)[:64, :]
    leaves_t = -sums_t[:32] / (sums_t[32:] + reg_lambda)
    leaves = jnp.transpose(leaves_t)
    for n in range(8):
        leaves_ref[n] = leaves[2 * n : 2 * n + 2, :]

    def update(i, carry):
        at = pl.ds(pl.multiple_of(i * LANE_BLOCK, LANE_BLOCK), LANE_BLOCK)
        count = flag_buf[0, :, at]
        for j in range(1, 8):
            count = count + flag_buf[j, :, at]
        slot = nodes_ref[:, at] * 2 + jnp.where(count > 0.5, 1, 0)
        slot_hot = jnp.where(iota16 == slot, one, zero).astype(jnp.bfloat16)
        new_ref[:, at] = logits_ref[:, at] + step_size * exact_dot(leaves_t, slot_hot, NN)
        return carry

    lax.fori_loop(0, rows // LANE_BLOCK, update, 0)

    after_y2(2)
    after_y2(3)
    after_z1(0)
    after_z1(1)
    after_z2(0)
    after_z2(1)

    lane_in = lax.broadcasted_iota(jnp.int32, (128, 128), 0)
    lane_out = lax.broadcasted_iota(jnp.int32, (128, 128), 1)
    same = (lane_in // BINS) == (lane_out // BINS)
    bin_in, bin_out = lane_in % BINS, lane_out % BINS
    as_weights = lambda mask: jnp.where(mask, one, zero).astype(jnp.bfloat16)
    lower = as_weights(same & (bin_in < bin_out) & (bin_in < BINS - 1))
    every = as_weights(same)
    last = as_weights(same & (bin_in == BINS - 1))
    lane = lax.broadcasted_iota(jnp.int32, (1, 128), 1)
    for colour in range(2):
        z3_copy(colour).wait_recv()
        k = 2 * z0 + colour
        owned = hist[2 * k + 1, z1, 2 * y + z2] + z3_buf[colour]
        left_base = exact_dot(owned, lower, NN)
        node_total = exact_dot(owned, every, NN)
        left_miss = left_base + exact_dot(owned, last, NN)
        parent = ratio(node_total)
        gain_left = (ratio(left_miss) + ratio(node_total - left_miss) - parent) / 64.0
        gain_right = (ratio(left_base) + ratio(node_total - left_base) - parent) / 64.0
        gain_ref[0, 2 * colour : 2 * colour + 1, :] = jnp.where(
            lane < BINS, gain_left, pltpu.roll(gain_right, BINS, 1)
        )
        gain_ref[0, 2 * colour + 1 : 2 * colour + 2, :] = jnp.where(
            lane < BINS, pltpu.roll(gain_left, BINS, 1), gain_right
        )

    for stage in (flags, stage1, stage2, stage3):
        stage[2]()
    for k in range(4):
        core_copy(k).wait_send()
        y1_copy(k, 0).wait_send()
        y1_copy(k, 1).wait_send()
        y2_copy(k).wait_send()
    for colour in range(2):
        z1_copy(colour).wait_send()
        z2_copy(colour).wait_send()
        z3_copy(colour).wait_send()


def local(logits, labels, node_ids, bin_codes, split_feature, split_bin, split_missing):
    rows = logits.shape[0]
    f32 = jnp.float32
    vmem = pl.BlockSpec(memory_space=pltpu.VMEM)
    smem = pl.BlockSpec(memory_space=pltpu.SMEM)
    dma = pltpu.SemaphoreType.DMA
    new_t, gains, leaves = pl.pallas_call(
        kernel,
        out_shape=(
            jax.ShapeDtypeStruct((32, rows), f32),
            jax.ShapeDtypeStruct((1, 4, 128), f32),
            jax.ShapeDtypeStruct((8, 2, 32), f32),
        ),
        in_specs=[smem] * 3 + [vmem] * 4,
        out_specs=(vmem, vmem, vmem),
        scratch_shapes=[
            pltpu.VMEM((512, rows), jnp.bfloat16),
            pltpu.VMEM((256, rows), jnp.bfloat16),
            pltpu.VMEM((8, 2, 8, 64, 128), f32),
            pltpu.VMEM((4, 2, 8, 64, 128), f32),
            pltpu.VMEM((4, 2, 2, 2, 64, 128), f32),
            pltpu.VMEM((4, 2, 2, 64, 128), f32),
            pltpu.VMEM((2, 2, 2, 64, 128), f32),
            pltpu.VMEM((2, 2, 64, 128), f32),
            pltpu.VMEM((2, 64, 128), f32),
            pltpu.VMEM((8, 1, rows), f32),
            pltpu.VMEM((8, 16, 128), f32),
            pltpu.VMEM((8, 16, 128), f32),
            pltpu.VMEM((8, 16, 128), f32),
            dma((4,)),
            dma((4,)),
            dma((4, 2)),
            dma((4, 2)),
            dma((4,)),
            dma((4,)),
        ]
        + [dma((2,))] * 6
        + [dma((7,)), dma((8,))] * 4,
        compiler_params=pltpu.CompilerParams(
            collective_id=0, has_side_effects=True, vmem_limit_bytes=48 * 1024 * 1024
        ),
    )(
        split_feature,
        split_bin,
        split_missing,
        logits.T,
        labels.reshape(1, rows),
        node_ids.reshape(1, rows),
        bin_codes.T,
    )
    return new_t.T, gains, leaves


def solution(mesh):
    return jax.shard_map(
        local,
        mesh=mesh,
        in_specs=(P("rows", None), P("rows"), P("rows"), P("rows", "feat"), P(), P(), P()),
        out_specs=(P("rows", None), P("rows", "feat", None), P()),
        check_vma=False,
    )
```

time: 614 us -> 71.1 us (0.12)
  the two profiles are of different devices: /device:TPU:1 before, /device:TPU:32 now
where the time goes in v1:
time: 71.1 us; the launch traced here: 70.8 us
  Pallas kernels  64.1 us (90%)
  local copies, waits for them, and re-layouts  5.99 us (8%)
    pallas_call x1, Pallas kernels, local(): pl.pallas_call(kernel, out_shape=(jax.ShapeDtypeStruct((32, rows), f32),...  64.1 us
    unnamed x17, local copies, waits for them, and re-layouts  5.99 us

profile of v1, /device:TPU:32, one launch (start us, length us, event | category | flops | bytes accessed | tf_op | source)
XLA Modules:
  0.0 70.8 jit_solution(18361262953130679674)
XLA Ops:
  0.6 0.0 copy-start.4
  0.6 0.0 copy-start.5
  0.7 0.0 copy-start.6
  0.7 0.6 copy-done.4
  1.3 0.0 copy-done.5
  1.3 0.0 copy-done.6
  1.3 0.0 copy-start
  1.3 1.0 %copy-done = f32[3072,32]{0,1:T(8,128)S(1)} copy-done((f32[3072,32]{0,1:T(8,128)S(1)}, f32[3072,32]{0,1:T(8,128)}, u32[]{:S(2)}) %copy-start) | copy-done | bytes 393240
  2.3 0.0 copy-start.1
  2.3 1.0 %copy-done.1 = s32[3072,32]{0,1:T(8,128)S(1)} copy-done((s32[3072,32]{0,1:T(8,128)S(1)}, s32[3072,32]{0,1:T(8,128)}, u32[]{:S(2)}) %copy-start.1) | copy-done | bytes 393240
  3.3 0.0 copy-start.2
  3.3 0.7 copy-done.2
  4.0 0.0 copy-start.3
  4.0 0.7 copy-done.3
  4.7 64.1 %shard_map.94 = (f32[32,3072]{1,0:T(8,128)S(1)}, f32[1,4,128]{2,1,0:T(4,128)S(1)}, f32[8,2,32]{2,1,0:T(2,128)S(1)}) custom-call(s32[8]{0:T(128)S(1)} %copy-done.4, s32[8]{0:T(128)S(1)} %copy-done.5, s32[8]{0:T(128)S(1)} %copy-done.6, f32[32,3072]{1,0:T(8,128)S(1)} %bitcast.6, s32[1,3072]{1,0:T(1,128)S(1)} %bitcast.8, s32[1,3072]{1,0:T(1,128)S(1)} %bitcast.9, ...), custom_call_target="tpu_custom_call" | custom-call | tf_op jit(solution)/shard_map/pallas_call | solution.py:428
  68.8 0.7 %copy.13 = f32[3072,32]{0,1:T(8,128)} copy(f32[3072,32]{0,1:T(8,128)S(1)} %bitcast.5) | data formatting | bytes 786432
  69.6 0.6 copy.14
  70.2 0.6 copy.15
Async XLA Ops:
  0.6 0.7 copy-start.4
  0.6 0.7 copy-start.5
  0.7 0.7 copy-start.6
  1.3 1.0 %copy-start = (f32[3072,32]{0,1:T(8,128)S(1)}, f32[3072,32]{0,1:T(8,128)}, u32[]{:S(2)}) copy-start(f32[3072,32]{0,1:T(8,128)} %param.7) | copy-start | bytes 1179652
  2.3 1.0 %copy-start.1 = (s32[3072,32]{0,1:T(8,128)S(1)}, s32[3072,32]{0,1:T(8,128)}, u32[]{:S(2)}) copy-start(s32[3072,32]{0,1:T(8,128)} %param.10) | copy-start | bytes 1179652
  3.3 0.7 copy-start.2
  4.0 0.7 copy-start.3

commit v2 on v1

v2 whole, which is shorter than its diff:
```python
import jax
import jax.numpy as jnp
from jax import lax
from jax.experimental import pallas as pl
from jax.experimental.pallas import tpu as pltpu
from jax.sharding import PartitionSpec as P

BINS = 64
MESH = pl.DeviceIdType.MESH
reg_lambda = 1.0
step_size = 0.3
LANE_BLOCK = 512
NT = (((1,), (1,)), ((), ()))
NN = (((1,), (0,)), ((), ()))


def split3(x):
    hi = x.astype(jnp.bfloat16)
    rest = x - hi.astype(jnp.float32)
    mid = rest.astype(jnp.bfloat16)
    low = (rest - mid.astype(jnp.float32)).astype(jnp.bfloat16)
    return hi, mid, low


def exact_dot(x, weights, dims):
    hi, mid, low = split3(x)
    dot = lambda part: lax.dot_general(part, weights, dims, preferred_element_type=jnp.float32)
    return dot(hi) + (dot(mid) + dot(low))


def ratio(sums):
    grad_part = sums[:32]
    hess_part = sums[32:]
    return jnp.sum(grad_part * grad_part / (hess_part + reg_lambda), axis=0, keepdims=True)


def kernel(
    feature_hbm,
    bin_hbm,
    missing_hbm,
    logits_hbm,
    labels_hbm,
    nodes_hbm,
    codes_hbm,
    new_hbm,
    gain_hbm,
    leaves_hbm,
    new_ref,
    gain_ref,
    leaves_ref,
    feature_ref,
    bin_ref,
    missing_ref,
    logits_ref,
    labels_ref,
    nodes_ref,
    codes_ref,
    masked,
    hot,
    hist,
    core_buf,
    y1_buf,
    y2_buf,
    z1_buf,
    direct_buf,
    flag_buf,
    far_flag,
    x_buf,
    group_buf,
    pair_buf,
    load_sem,
    store_sem,
    core_send,
    core_recv,
    y1_send,
    y1_recv,
    y2_send,
    y2_recv,
    z1_send,
    z1_recv,
    direct_send,
    direct_recv,
    flag_send,
    flag_recv,
    far_send,
    far_recv,
    x_send,
    x_recv,
    group_send,
    group_recv,
    pair_send,
    pair_recv,
    vouch4,
    vouch2,
):
    rows = logits_ref.shape[1]
    row = lax.axis_index("rows")
    feat = lax.axis_index("feat")
    core = row % 2
    z = (row // 2) % 8
    y = row // 16
    x, z_hi = feat // 2, feat % 2
    z0, z1, z2 = z % 2, (z // 2) % 2, z // 4
    quad = z // 2
    group = y * 2 + core
    ya = y + 1 - 2 * (y % 2)
    yb = 3 - y
    yc = 3 - ya

    loads = [
        pltpu.make_async_copy(src, dst, load_sem.at[i])
        for i, (src, dst) in enumerate(
            (
                (logits_hbm, logits_ref),
                (labels_hbm, labels_ref),
                (nodes_hbm, nodes_ref),
                (codes_hbm, codes_ref),
                (feature_hbm, feature_ref),
                (bin_hbm, bin_ref),
                (missing_hbm, missing_ref),
            )
        )
    ]
    for load in loads:
        load.start()
    stores = [
        pltpu.make_async_copy(src, dst, store_sem.at[i])
        for i, (src, dst) in enumerate(
            ((new_ref, new_hbm), (leaves_ref, leaves_hbm), (gain_ref, gain_hbm))
        )
    ]

    def at_y(other):
        return (other * 16 + z * 2 + core, feat)

    def at_z(other):
        return (y * 16 + other * 2 + core, feat)

    core_peer = (row + 1 - 2 * core, feat)
    z_peer1 = at_z(z + 1 - 2 * z0)
    z_peer2 = at_z(z + 2 - 4 * z1)
    z_peer4 = at_z(z + 4 - 8 * z2)
    far_peer = (row, x * 2 + 1 - z_hi)
    ring4 = (y * 16 + ((z + 4) % 8) * 2 + core, x * 2 + 1 - z_hi)

    def x_peer(d):
        return (row, ((x + d) % 4) * 2 + z_hi)

    def group_peer(d):
        other = (group + d) % 8
        return ((other // 2) * 16 + z * 2 + other % 2, feat)

    def signal(sem, peer):
        pl.semaphore_signal(sem, inc=1, device_id=peer, device_id_type=MESH)

    barrier = pltpu.get_barrier_semaphore()
    greeted = [ring4, z_peer4, z_peer2, z_peer1]
    greeted += [x_peer(d) for d in range(1, 4)] + [group_peer(d) for d in range(1, 8)]
    for peer in greeted:
        signal(barrier, peer)

    iota16 = lax.broadcasted_iota(jnp.int32, (16, LANE_BLOCK), 0)
    iota32 = lax.broadcasted_iota(jnp.int32, (32, LANE_BLOCK), 0)
    one, zero = jnp.float32(1.0), jnp.float32(0.0)

    for load in loads:
        load.wait()

    def prepare(i, side_sums):
        at = pl.ds(pl.multiple_of(i * LANE_BLOCK, LANE_BLOCK), LANE_BLOCK)
        expo = jnp.exp(logits_ref[:, at])
        prob = expo / jnp.sum(expo, axis=0, keepdims=True)
        target = jnp.where(iota32 == labels_ref[:, at], one, zero)
        grad = (prob - target).astype(jnp.bfloat16).astype(jnp.float32)
        hess = (prob * (1.0 - prob)).astype(jnp.bfloat16).astype(jnp.float32)
        both = jnp.concatenate([grad, hess], axis=0)
        node = nodes_ref[:, at]
        row_feature = jnp.zeros_like(node)
        row_bin = jnp.zeros_like(node)
        row_missing = jnp.zeros_like(node)
        for n in range(8):
            here = node == n
            masked[n * 64 : (n + 1) * 64, at] = jnp.where(here, both, zero).astype(jnp.bfloat16)
            row_feature = jnp.where(here, feature_ref[n], row_feature)
            row_bin = jnp.where(here, bin_ref[n], row_bin)
            row_missing = jnp.where(here, missing_ref[n], row_missing)
        column = row_feature - feat * 32
        owned = (column >= 0) & (column < 32)
        code = jnp.sum(
            jnp.where(iota32 == column, codes_ref[:, at].astype(jnp.float32), zero),
            axis=0,
            keepdims=True,
        ).astype(jnp.int32)
        left = (code < row_bin) | ((code == BINS - 1) & (row_missing == 1))
        right = jnp.where(left, 0, 1)
        flag_buf[x, :, at] = jnp.where(owned, right, 0).astype(jnp.float32)
        slot = jnp.where(owned, node * 2 + right, -1)
        slot_hot = jnp.where(iota16 == slot, one, zero).astype(jnp.bfloat16)
        return side_sums + lax.dot_general(
            slot_hot, both.astype(jnp.bfloat16), NT, preferred_element_type=jnp.float32
        )

    side_sums = lax.fori_loop(
        0, rows // LANE_BLOCK, prepare, jnp.zeros((16, 64), jnp.float32)
    )
    x_buf[x] = jnp.concatenate([side_sums, jnp.zeros((16, 64), jnp.float32)], axis=1)

    def remote(src, dst, send, recv, peer):
        return pltpu.make_async_remote_copy(
            src_ref=src,
            dst_ref=dst,
            send_sem=send,
            recv_sem=recv,
            device_id=peer,
            device_id_type=MESH,
        )

    def exchange(buf, send, recv, mine, count, peer):
        def copy(d, slot):
            return remote(buf.at[slot], buf.at[slot], send.at[d - 1], recv.at[slot], peer(d))

        def start():
            for d in range(1, count):
                copy(d, mine).start()

        def arrive():
            for d in range(1, count):
                copy(d, (mine + d) % count).wait_recv()

        def finish():
            for d in range(1, count):
                copy(d, mine).wait_send()

        return start, arrive, finish

    flags = exchange(flag_buf, flag_send, flag_recv, x, 4, x_peer)
    along_x = exchange(x_buf, x_send, x_recv, x, 4, x_peer)
    in_group = exchange(group_buf, group_send, group_recv, group, 8, group_peer)
    pair_peers = (z_peer1, z_peer2, z_peer4, far_peer)

    def pair_copy(i):
        return remote(
            pair_buf.at[i, 0], pair_buf.at[i, 1], pair_send.at[i], pair_recv.at[i], pair_peers[i]
        )

    far_copy = remote(far_flag.at[0], far_flag.at[1], far_send.at[0], far_recv.at[0], far_peer)

    def total(buf, count):
        sums = buf[0]
        for i in range(1, count):
            sums = sums + buf[i]
        return sums

    def after_x():
        along_x[1]()
        group_buf[group] = total(x_buf, 4)
        in_group[0]()

    def after_group():
        in_group[1]()
        pair_buf[0, 0] = total(group_buf, 8)
        pair_copy(0).start()

    def after_pair(i):
        pair_copy(i).wait_recv()
        pair_buf[i + 1, 0] = pair_buf[i, 0] + pair_buf[i, 1]
        pair_copy(i + 1).start()

    def core_copy(k):
        return remote(
            hist.at[2 * k], core_buf.at[k], core_send.at[k], core_recv.at[k], core_peer
        )

    first_y = (ya, yb)
    second_y = (yb, ya)

    def part_of(k, dest, colour):
        return hist.at[2 * k + 1, :, pl.ds(2 * dest, 2), pl.ds(32 * colour, 32)]

    def y1_copy(k, colour, part):
        dest = first_y[colour] if part else yc
        return remote(
            part_of(k, dest, colour),
            y1_buf.at[k, colour, part],
            y1_send.at[k, colour, part],
            y1_recv.at[k, colour, part],
            at_y(first_y[colour]),
        )

    def y2_copy(k, colour):
        dest = second_y[colour]
        return remote(
            part_of(k, dest, colour),
            y2_buf.at[k, colour],
            y2_send.at[k, colour],
            y2_recv.at[k, colour],
            at_y(dest),
        )

    def z1_copy(k, colour):
        return remote(
            part_of(k, y, colour),
            z1_buf.at[k // 2, colour],
            z1_send.at[k // 2, colour],
            z1_recv.at[k // 2, colour],
            z_peer1,
        )

    def direct_copy(k, colour, d):
        other = (quad + d) % 4
        return remote(
            hist.at[2 * k + 1, other % 2, 2 * y + other // 2, pl.ds(32 * colour, 32)],
            direct_buf.at[k // 2, colour, d - 1],
            direct_send.at[k // 2, colour, d - 1],
            direct_recv.at[k // 2, colour, d - 1],
            at_z(other * 2 + z0),
        )

    iota64 = lax.broadcasted_iota(jnp.int32, (64, rows), 0)

    def after_core(k):
        core_copy(k).wait_recv()
        hist[2 * k + 1] = hist[2 * k + 1] + core_buf[k]

    def send_y1(k):
        for part in range(2):
            for colour in range(2):
                y1_copy(k, colour, part).start()

    def step(s, carry):
        k = s // 2
        side = s % 2
        half, pair = k % 2, k // 2
        owner = side * core + (1 - side) * (1 - core)
        base = half * 8 + owner * 4 + pair * 2
        for high in range(2):
            for low in range(2):
                code = codes_ref[pl.ds(base + 16 * high + low, 1), :]
                start = (high * 2 + low) * 64
                hot[start : start + 64, :] = jnp.where(code == iota64, one, zero).astype(
                    jnp.bfloat16
                )
        out = lax.dot_general(masked[...], hot[...], NT, preferred_element_type=jnp.float32)
        for high in range(2):
            for n in range(8):
                hist[s, high, n] = out[n * 64 : (n + 1) * 64, high * 128 : (high + 1) * 128]

        @pl.when(s == 0)
        def _():
            pl.semaphore_wait(barrier, len(greeted))
            signal(vouch4, ring4)
            signal(vouch4, z_peer4)
            signal(vouch2, z_peer2)

        @pl.when(side == 0)
        def _():
            core_copy(k).start()

        @pl.when(s == 0)
        def _():
            along_x[0]()
            flags[0]()

        @pl.when((side == 0) & (k > 0))
        def _():
            after_core(k - 1)

        @pl.when((side == 0) & (k > 0) & (k < 3))
        def _():
            send_y1(k - 1)

        @pl.when(s == 3)
        def _():
            after_x()

        @pl.when(s == 7)
        def _():
            after_group()

        return carry

    lax.fori_loop(0, 8, step, 0)

    def add_part(k, dest, colour, incoming):
        at = pl.ds(2 * dest, 2)
        lines = slice(32 * colour, 32 * colour + 32)
        hist[2 * k + 1, :, at, lines] = hist[2 * k + 1, :, at, lines] + incoming

    def after_y1(k):
        for colour in range(2):
            y1_copy(k, colour, 0).wait_recv()
            add_part(k, second_y[colour], colour, y1_buf[k, colour, 0])
            y2_copy(k, colour).start()
        for colour in range(2):
            y1_copy(k, colour, 1).wait_recv()
            add_part(k, y, colour, y1_buf[k, colour, 1])

    def after_y2(k):
        for colour in range(2):
            y2_copy(k, colour).wait_recv()
            add_part(k, y, colour, y2_buf[k, colour])

            @pl.when(z0 != k % 2)
            def _():
                z1_copy(k, colour).start()

    def after_z1(k):
        @pl.when(z0 == k % 2)
        def _():
            for colour in range(2):
                z1_copy(k, colour).wait_recv()
                add_part(k, y, colour, z1_buf[k // 2, colour])
                for d in (2, 1, 3):
                    direct_copy(k, colour, d).start()

    after_y1(0)
    send_y1(2)
    after_core(3)
    pl.semaphore_wait(vouch4, 2)
    pl.semaphore_wait(vouch2, 1)
    flags[1]()
    far_flag[0] = total(flag_buf, 4)
    far_copy.start()
    after_y1(1)
    send_y1(3)
    after_pair(0)
    after_y2(0)
    after_y1(2)
    after_pair(1)
    after_y2(1)
    after_z1(0)
    after_y1(3)
    after_y2(2)
    after_pair(2)
    after_z1(1)
    after_y2(3)
    after_z1(2)
    after_z1(3)

    pair_copy(3).wait_recv()
    sums_t = jnp.transpose(pair_buf[3, 0] + pair_buf[3, 1])[:64, :]
    leaves_t = -sums_t[:32] / (sums_t[32:] + reg_lambda)
    leaves = jnp.transpose(leaves_t)
    for n in range(8):
        leaves_ref[n] = leaves[2 * n : 2 * n + 2, :]
    far_copy.wait_recv()

    def update(i, carry):
        at = pl.ds(pl.multiple_of(i * LANE_BLOCK, LANE_BLOCK), LANE_BLOCK)
        count = far_flag[0, :, at] + far_flag[1, :, at]
        slot = nodes_ref[:, at] * 2 + jnp.where(count > 0.5, 1, 0)
        slot_hot = jnp.where(iota16 == slot, one, zero).astype(jnp.bfloat16)
        new_ref[:, at] = logits_ref[:, at] + step_size * exact_dot(leaves_t, slot_hot, NN)
        return carry

    lax.fori_loop(0, rows // LANE_BLOCK, update, 0)
    stores[0].start()
    stores[1].start()

    lane_in = lax.broadcasted_iota(jnp.int32, (128, 128), 0)
    lane_out = lax.broadcasted_iota(jnp.int32, (128, 128), 1)
    same = (lane_in // BINS) == (lane_out // BINS)
    bin_in, bin_out = lane_in % BINS, lane_out % BINS
    as_weights = lambda mask: jnp.where(mask, one, zero).astype(jnp.bfloat16)
    lower = as_weights(same & (bin_in < bin_out) & (bin_in < BINS - 1))
    every = as_weights(same)
    last = as_weights(same & (bin_in == BINS - 1))
    lane = lax.broadcasted_iota(jnp.int32, (1, 128), 1)
    for pair in range(2):
        k = 2 * pair + z0
        parts = []
        for colour in range(2):
            part = hist[2 * k + 1, z1, 2 * y + z2, 32 * colour : 32 * colour + 32]
            for d in (2, 1, 3):
                direct_copy(k, colour, d).wait_recv()
                part = part + direct_buf[pair, colour, d - 1]
            parts.append(part)
        owned = jnp.concatenate(parts, axis=0)
        left_base = exact_dot(owned, lower, NN)
        node_total = exact_dot(owned, every, NN)
        left_miss = left_base + exact_dot(owned, last, NN)
        parent = ratio(node_total)
        gain_left = (ratio(left_miss) + ratio(node_total - left_miss) - parent) / 64.0
        gain_right = (ratio(left_base) + ratio(node_total - left_base) - parent) / 64.0
        gain_ref[0, 2 * pair : 2 * pair + 1, :] = jnp.where(
            lane < BINS, gain_left, pltpu.roll(gain_right, BINS, 1)
        )
        gain_ref[0, 2 * pair + 1 : 2 * pair + 2, :] = jnp.where(
            lane < BINS, pltpu.roll(gain_left, BINS, 1), gain_right
        )

    stores[2].start()
    for stage in (flags, along_x, in_group):
        stage[2]()
    far_copy.wait_send()
    for i in range(4):
        pair_copy(i).wait_send()
    for k in range(4):
        core_copy(k).wait_send()
        for colour in range(2):
            y1_copy(k, colour, 0).wait_send()
            y1_copy(k, colour, 1).wait_send()
            y2_copy(k, colour).wait_send()
    for pair in range(2):
        for colour in range(2):
            z1_copy(2 * pair + 1 - z0, colour).wait_send()
            for d in (1, 2, 3):
                direct_copy(2 * pair + z0, colour, d).wait_send()
    for store in stores:
        store.wait()


def move(new_ref, gain_ref, leaves_ref, new_out, gain_out, leaves_out, new_held, gain_held, leaves_held, sems):
    width = new_ref.shape[1] // 4
    parts = [(leaves_ref, leaves_held, leaves_out), (gain_ref, gain_held, gain_out)]
    for i in range(4):
        at = (slice(None), pl.ds(i * width, width))
        parts.append((new_ref.at[at], new_held.at[at], new_out.at[at]))
    loads = [pltpu.make_async_copy(a, b, sems.at[0, i]) for i, (a, b, _) in enumerate(parts)]
    stores = [pltpu.make_async_copy(b, c, sems.at[1, i]) for i, (_, b, c) in enumerate(parts)]
    for load in loads:
        load.start()
    for load, store in zip(loads, stores):
        load.wait()
        store.start()
    for store in stores:
        store.wait()


def local(logits, labels, node_ids, bin_codes, split_feature, split_bin, split_missing):
    rows = logits.shape[0]
    f32, i32 = jnp.float32, jnp.int32
    hbm = pl.BlockSpec(memory_space=pl.ANY)
    dma = pltpu.SemaphoreType.DMA
    out_shape = (
        jax.ShapeDtypeStruct((32, rows), f32),
        jax.ShapeDtypeStruct((1, 4, 128), f32),
        jax.ShapeDtypeStruct((8, 2, 32), f32),
    )
    results = pl.pallas_call(
        kernel,
        out_shape=out_shape,
        in_specs=[hbm] * 7,
        out_specs=(hbm, hbm, hbm),
        scratch_shapes=[
            pltpu.VMEM((32, rows), f32),
            pltpu.VMEM((1, 4, 128), f32),
            pltpu.VMEM((8, 2, 32), f32),
            pltpu.SMEM((8,), i32),
            pltpu.SMEM((8,), i32),
            pltpu.SMEM((8,), i32),
            pltpu.VMEM((32, rows), f32),
            pltpu.VMEM((1, rows), i32),
            pltpu.VMEM((1, rows), i32),
            pltpu.VMEM((32, rows), i32),
            pltpu.VMEM((512, rows), jnp.bfloat16),
            pltpu.VMEM((256, rows), jnp.bfloat16),
            pltpu.VMEM((8, 2, 8, 64, 128), f32),
            pltpu.VMEM((4, 2, 8, 64, 128), f32),
            pltpu.VMEM((4, 2, 2, 2, 2, 32, 128), f32),
            pltpu.VMEM((4, 2, 2, 2, 32, 128), f32),
            pltpu.VMEM((2, 2, 2, 2, 32, 128), f32),
            pltpu.VMEM((2, 2, 3, 32, 128), f32),
            pltpu.VMEM((4, 1, rows), f32),
            pltpu.VMEM((2, 1, rows), f32),
            pltpu.VMEM((4, 16, 128), f32),
            pltpu.VMEM((8, 16, 128), f32),
            pltpu.VMEM((4, 2, 16, 128), f32),
            dma((7,)),
            dma((3,)),
            dma((4,)),
            dma((4,)),
            dma((4, 2, 2)),
            dma((4, 2, 2)),
            dma((4, 2)),
            dma((4, 2)),
            dma((2, 2)),
            dma((2, 2)),
            dma((2, 2, 3)),
            dma((2, 2, 3)),
            dma((3,)),
            dma((4,)),
            dma((1,)),
            dma((1,)),
            dma((3,)),
            dma((4,)),
            dma((7,)),
            dma((8,)),
            dma((4,)),
            dma((4,)),
            pltpu.SemaphoreType.REGULAR,
            pltpu.SemaphoreType.REGULAR,
        ],
        compiler_params=pltpu.CompilerParams(
            collective_id=0, has_side_effects=True, vmem_limit_bytes=56 * 1024 * 1024
        ),
    )(
        split_feature,
        split_bin,
        split_missing,
        logits.T,
        labels.reshape(1, rows),
        node_ids.reshape(1, rows),
        bin_codes.T,
    )
    new_t, gains, leaves = pl.pallas_call(
        move,
        out_shape=out_shape,
        in_specs=[hbm] * 3,
        out_specs=(hbm, hbm, hbm),
        scratch_shapes=[
            pltpu.VMEM((32, rows), f32),
            pltpu.VMEM((1, 4, 128), f32),
            pltpu.VMEM((8, 2, 32), f32),
            dma((2, 6)),
        ],
    )(*results)
    return new_t.T, gains, leaves


def solution(mesh):
    return jax.shard_map(
        local,
        mesh=mesh,
        in_specs=(P("rows", None), P("rows"), P("rows"), P("rows", "feat"), P(), P(), P()),
        out_specs=(P("rows", None), P("rows", "feat", None), P()),
        check_vma=False,
    )
```

time: 71.1 us -> 55.1 us (0.77)
  Pallas kernels: 64.1 us -> 54.2 us
  local copies, waits for them, and re-layouts: 5.99 us -> 0 us
    pallas_call x1 -> x2, Pallas kernels: 64.1 us -> 54.2 us  [the longest x1 52.4 us: local(): pl.pallas_call(kernel, out_shape=out_shape, in_specs=[hbm] * 7, out_specs...]
    unnamed x17 -> x0, local copies, waits for them, and re-layouts: 5.99 us -> none
where the time goes in v2:
time: 55.1 us; the launch traced here: 54.9 us
  Pallas kernels  54.2 us (98%)
  between operations  0.64 us (1%)
    pallas_call x1, Pallas kernels, local(): pl.pallas_call(kernel, out_shape=out_shape, in_specs=[hbm] * 7, out_specs...  52.4 us
    pallas_call x1, Pallas kernels, local(): pl.pallas_call(move, out_shape=out_shape, in_specs=[hbm] * 3, out_specs=(...  1.8 us

profile of v2, /device:TPU:32, one launch (start us, length us, event | category | flops | bytes accessed | tf_op | source)
XLA Modules:
  0.0 54.9 jit_solution(1930148576679118655)
XLA Ops:
  0.6 52.4 %shard_map.94 = (f32[32,3072]{1,0:T(8,128)}, f32[1,4,128]{2,1,0:T(4,128)}, f32[8,2,32]{2,1,0:T(2,128)}) custom-call(s32[8]{0:T(128)} %feature_hbm.1, s32[8]{0:T(128)} %bin_hbm.1, s32[8]{0:T(128)} %missing_hbm.1, f32[32,3072]{1,0:T(8,128)} %bitcast.5, s32[1,3072]{1,0:T(1,128)} %bitcast.7, s32[1,3072]{1,0:T(1,128)} %bitcast.8, s32[32,3072]{1,0:T(8,128)} %bitcast.6), custom_call_target="tpu_custom_call" | custom-call | tf_op jit(solution)/shard_map/pallas_call | solution.py:540
  53.1 1.8 %shard_map.95 = (f32[32,3072]{1,0:T(8,128)}, f32[1,4,128]{2,1,0:T(4,128)}, f32[8,2,32]{2,1,0:T(2,128)}) custom-call(f32[32,3072]{1,0:T(8,128)} %get-tuple-element.9.new_ref, f32[1,4,128]{2,1,0:T(4,128)} %get-tuple-element.10.gain_ref, f32[8,2,32]{2,1,0:T(2,128)} %get-tuple-element.11.leaves_ref), custom_call_target="tpu_custom_call" | custom-call | tf_op jit(solution)/shard_map/pallas_call | solution.py:606

commit v3 on v2

--- a/solution.py
+++ b/solution.py
@@ -68,6 +68,7 @@
     x_buf,
     group_buf,
     pair_buf,
+    wide_buf,
     load_sem,
     store_sem,
     core_send,
@@ -90,6 +91,8 @@
     group_recv,
     pair_send,
     pair_recv,
+    wide_send,
+    wide_recv,
     vouch4,
     vouch2,
 ):
@@ -102,7 +105,8 @@
     x, z_hi = feat // 2, feat % 2
     z0, z1, z2 = z % 2, (z // 2) % 2, z // 4
     quad = z // 2
-    group = y * 2 + core
+    group = (y * 2 + core) * 2 + z0
+    wide = z_hi * 2 + z2
     ya = y + 1 - 2 * (y % 2)
     yb = 3 - y
     yc = 3 - ya
@@ -147,15 +151,19 @@
         return (row, ((x + d) % 4) * 2 + z_hi)
 
     def group_peer(d):
-        other = (group + d) % 8
-        return ((other // 2) * 16 + z * 2 + other % 2, feat)
+        other = (group + d) % 16
+        return ((other // 4) * 16 + (z - z0 + other % 2) * 2 + (other // 2) % 2, feat)
+
+    def wide_peer(d):
+        other = (wide + d) % 4
+        return (y * 16 + (z % 4 + 4 * (other % 2)) * 2 + core, x * 2 + other // 2)
 
     def signal(sem, peer):
         pl.semaphore_signal(sem, inc=1, device_id=peer, device_id_type=MESH)
 
     barrier = pltpu.get_barrier_semaphore()
-    greeted = [ring4, z_peer4, z_peer2, z_peer1]
-    greeted += [x_peer(d) for d in range(1, 4)] + [group_peer(d) for d in range(1, 8)]
+    greeted = [ring4, z_peer4, z_peer2]
+    greeted += [x_peer(d) for d in range(1, 4)] + [group_peer(d) for d in range(1, 16)]
     for peer in greeted:
         signal(barrier, peer)
 
@@ -203,7 +211,7 @@
     side_sums = lax.fori_loop(
         0, rows // LANE_BLOCK, prepare, jnp.zeros((16, 64), jnp.float32)
     )
-    x_buf[x] = jnp.concatenate([side_sums, jnp.zeros((16, 64), jnp.float32)], axis=1)
+    x_buf[x] = jnp.concatenate([side_sums[:8], side_sums[8:]], axis=1)
 
     def remote(src, dst, send, recv, peer):
         return pltpu.make_async_remote_copy(
@@ -235,14 +243,11 @@
 
     flags = exchange(flag_buf, flag_send, flag_recv, x, 4, x_peer)
     along_x = exchange(x_buf, x_send, x_recv, x, 4, x_peer)
-    in_group = exchange(group_buf, group_send, group_recv, group, 8, group_peer)
-    pair_peers = (z_peer1, z_peer2, z_peer4, far_peer)
-
-    def pair_copy(i):
-        return remote(
-            pair_buf.at[i, 0], pair_buf.at[i, 1], pair_send.at[i], pair_recv.at[i], pair_peers[i]
-        )
-
+    in_group = exchange(group_buf, group_send, group_recv, group, 16, group_peer)
+    along_z = exchange(wide_buf, wide_send, wide_recv, wide, 4, wide_peer)
+    pair_copy = remote(
+        pair_buf.at[0], pair_buf.at[1], pair_send.at[0], pair_recv.at[0], z_peer2
+    )
     far_copy = remote(far_flag.at[0], far_flag.at[1], far_send.at[0], far_recv.at[0], far_peer)
 
     def total(buf, count):
@@ -258,13 +263,13 @@
 
     def after_group():
         in_group[1]()
-        pair_buf[0, 0] = total(group_buf, 8)
-        pair_copy(0).start()
-
-    def after_pair(i):
-        pair_copy(i).wait_recv()
-        pair_buf[i + 1, 0] = pair_buf[i, 0] + pair_buf[i, 1]
-        pair_copy(i + 1).start()
+        pair_buf[0] = total(group_buf, 16)
+        pair_copy.start()
+
+    def after_pair():
+        pair_copy.wait_recv()
+        wide_buf[wide] = pair_buf[0] + pair_buf[1]
+        along_z[0]()
 
     def core_copy(k):
         return remote(
@@ -274,32 +279,33 @@
     first_y = (ya, yb)
     second_y = (yb, ya)
 
-    def part_of(k, dest, colour):
-        return hist.at[2 * k + 1, :, pl.ds(2 * dest, 2), pl.ds(32 * colour, 32)]
-
-    def y1_copy(k, colour, part):
+    def part_of(u, dest, colour):
+        lines = pl.ds(32 * (u % 2) + 16 * colour, 16)
+        return hist.at[2 * (u // 2) + 1, :, pl.ds(2 * dest, 2), lines]
+
+    def y1_copy(u, colour, part):
         dest = first_y[colour] if part else yc
         return remote(
-            part_of(k, dest, colour),
-            y1_buf.at[k, colour, part],
-            y1_send.at[k, colour, part],
-            y1_recv.at[k, colour, part],
+            part_of(u, dest, colour),
+            y1_buf.at[u, colour, part],
+            y1_send.at[u, colour, part],
+            y1_recv.at[u, colour, part],
             at_y(first_y[colour]),
         )
 
-    def y2_copy(k, colour):
+    def y2_copy(u, colour):
         dest = second_y[colour]
         return remote(
-            part_of(k, dest, colour),
-            y2_buf.at[k, colour],
-            y2_send.at[k, colour],
-            y2_recv.at[k, colour],
+            part_of(u, dest, colour),
+            y2_buf.at[u, colour],
+            y2_send.at[u, colour],
+            y2_recv.at[u, colour],
             at_y(dest),
         )
 
     def z1_copy(k, colour):
         return remote(
-            part_of(k, y, colour),
+            hist.at[2 * k + 1, :, pl.ds(2 * y, 2), pl.ds(32 * colour, 32)],
             z1_buf.at[k // 2, colour],
             z1_send.at[k // 2, colour],
             z1_recv.at[k // 2, colour],
@@ -322,10 +328,45 @@
         core_copy(k).wait_recv()
         hist[2 * k + 1] = hist[2 * k + 1] + core_buf[k]
 
-    def send_y1(k):
+    def send_y1(u):
         for part in range(2):
             for colour in range(2):
-                y1_copy(k, colour, part).start()
+                y1_copy(u, colour, part).start()
+
+    def add_lines(k, dest, first, count, incoming):
+        at = (2 * k + 1, slice(None), pl.ds(2 * dest, 2), slice(first, first + count))
+        hist[at] = hist[at] + incoming
+
+    def add_part(u, dest, colour, incoming):
+        add_lines(u // 2, dest, 32 * (u % 2) + 16 * colour, 16, incoming)
+
+    def after_y1(u):
+        for colour in range(2):
+            y1_copy(u, colour, 0).wait_recv()
+            add_part(u, second_y[colour], colour, y1_buf[u, colour, 0])
+            y2_copy(u, colour).start()
+        for colour in range(2):
+            y1_copy(u, colour, 1).wait_recv()
+            add_part(u, y, colour, y1_buf[u, colour, 1])
+
+    def after_y2(u):
+        for colour in range(2):
+            y2_copy(u, colour).wait_recv()
+            add_part(u, y, colour, y2_buf[u, colour])
+
+        @pl.when(z0 != (u // 2) % 2)
+        def _():
+            z1_copy(u // 2, u % 2).start()
+
+    def after_z1(u):
+        k, half = u // 2, u % 2
+
+        @pl.when(z0 == k % 2)
+        def _():
+            z1_copy(k, half).wait_recv()
+            add_lines(k, y, 32 * half, 32, z1_buf[k // 2, half])
+            for d in (2, 1, 3):
+                direct_copy(k, half, d).start()
 
     def step(s, carry):
         k = s // 2
@@ -365,14 +406,29 @@
         def _():
             after_core(k - 1)
 
-        @pl.when((side == 0) & (k > 0) & (k < 3))
-        def _():
-            send_y1(k - 1)
+        @pl.when(s == 2)
+        def _():
+            send_y1(0)
+            send_y1(1)
 
         @pl.when(s == 3)
         def _():
             after_x()
 
+        @pl.when(s == 4)
+        def _():
+            send_y1(2)
+
+        @pl.when(s == 5)
+        def _():
+            after_y1(0)
+            send_y1(3)
+
+        @pl.when(s == 6)
+        def _():
+            after_y1(1)
+            send_y1(4)
+
         @pl.when(s == 7)
         def _():
             after_group()
@@ -381,64 +437,34 @@
 
     lax.fori_loop(0, 8, step, 0)
 
-    def add_part(k, dest, colour, incoming):
-        at = pl.ds(2 * dest, 2)
-        lines = slice(32 * colour, 32 * colour + 32)
-        hist[2 * k + 1, :, at, lines] = hist[2 * k + 1, :, at, lines] + incoming
-
-    def after_y1(k):
-        for colour in range(2):
-            y1_copy(k, colour, 0).wait_recv()
-            add_part(k, second_y[colour], colour, y1_buf[k, colour, 0])
-            y2_copy(k, colour).start()
-        for colour in range(2):
-            y1_copy(k, colour, 1).wait_recv()
-            add_part(k, y, colour, y1_buf[k, colour, 1])
-
-    def after_y2(k):
-        for colour in range(2):
-            y2_copy(k, colour).wait_recv()
-            add_part(k, y, colour, y2_buf[k, colour])
-
-            @pl.when(z0 != k % 2)
-            def _():
-                z1_copy(k, colour).start()
-
-    def after_z1(k):
-        @pl.when(z0 == k % 2)
-        def _():
-            for colour in range(2):
-                z1_copy(k, colour).wait_recv()
-                add_part(k, y, colour, z1_buf[k // 2, colour])
-                for d in (2, 1, 3):
-                    direct_copy(k, colour, d).start()
-
-    after_y1(0)
-    send_y1(2)
-    after_core(3)
-    pl.semaphore_wait(vouch4, 2)
-    pl.semaphore_wait(vouch2, 1)
-    flags[1]()
-    far_flag[0] = total(flag_buf, 4)
-    far_copy.start()
-    after_y1(1)
-    send_y1(3)
-    after_pair(0)
-    after_y2(0)
-    after_y1(2)
-    after_pair(1)
-    after_y2(1)
-    after_z1(0)
-    after_y1(3)
-    after_y2(2)
-    after_pair(2)
-    after_z1(1)
-    after_y2(3)
-    after_z1(2)
-    after_z1(3)
-
-    pair_copy(3).wait_recv()
-    sums_t = jnp.transpose(pair_buf[3, 0] + pair_buf[3, 1])[:64, :]
+    for u in range(2, 8):
+        after_y1(u)
+        if u == 2:
+            after_core(3)
+        if u + 3 < 8:
+            send_y1(u + 3)
+        after_y2(u - 2)
+        if u == 2:
+            pl.semaphore_wait(vouch4, 2)
+            pl.semaphore_wait(vouch2, 1)
+            flags[1]()
+            far_flag[0] = total(flag_buf, 4)
+            far_copy.start()
+        if u == 3:
+            after_pair()
+        if u >= 4:
+            after_z1(u - 4)
+    after_y2(6)
+    after_z1(4)
+    after_y2(7)
+    after_z1(5)
+    after_z1(6)
+    after_z1(7)
+
+    along_z[1]()
+    sums = total(wide_buf, 4)
+    sums = jnp.concatenate([sums, pltpu.roll(sums, 64, 1)], axis=0)
+    sums_t = jnp.transpose(sums)[:64, :]
     leaves_t = -sums_t[:32] / (sums_t[32:] + reg_lambda)
     leaves = jnp.transpose(leaves_t)
     for n in range(8):
@@ -490,17 +516,17 @@
         )
 
     stores[2].start()
-    for stage in (flags, along_x, in_group):
+    for stage in (flags, along_x, in_group, along_z):
         stage[2]()
     far_copy.wait_send()
-    for i in range(4):
-        pair_copy(i).wait_send()
+    pair_copy.wait_send()
     for k in range(4):
         core_copy(k).wait_send()
+    for u in range(8):
         for colour in range(2):
-            y1_copy(k, colour, 0).wait_send()
-            y1_copy(k, colour, 1).wait_send()
-            y2_copy(k, colour).wait_send()
+            y1_copy(u, colour, 0).wait_send()
+            y1_copy(u, colour, 1).wait_send()
+            y2_copy(u, colour).wait_send()
     for pair in range(2):
         for colour in range(2):
             z1_copy(2 * pair + 1 - z0, colour).wait_send()
@@ -557,23 +583,24 @@
             pltpu.VMEM((256, rows), jnp.bfloat16),
             pltpu.VMEM((8, 2, 8, 64, 128), f32),
             pltpu.VMEM((4, 2, 8, 64, 128), f32),
-            pltpu.VMEM((4, 2, 2, 2, 2, 32, 128), f32),
-            pltpu.VMEM((4, 2, 2, 2, 32, 128), f32),
+            pltpu.VMEM((8, 2, 2, 2, 2, 16, 128), f32),
+            pltpu.VMEM((8, 2, 2, 2, 16, 128), f32),
             pltpu.VMEM((2, 2, 2, 2, 32, 128), f32),
             pltpu.VMEM((2, 2, 3, 32, 128), f32),
             pltpu.VMEM((4, 1, rows), f32),
             pltpu.VMEM((2, 1, rows), f32),
-            pltpu.VMEM((4, 16, 128), f32),
-            pltpu.VMEM((8, 16, 128), f32),
-            pltpu.VMEM((4, 2, 16, 128), f32),
+            pltpu.VMEM((4, 8, 128), f32),
+            pltpu.VMEM((16, 8, 128), f32),
+            pltpu.VMEM((2, 8, 128), f32),
+            pltpu.VMEM((4, 8, 128), f32),
             dma((7,)),
             dma((3,)),
             dma((4,)),
             dma((4,)),
-            dma((4, 2, 2)),
-            dma((4, 2, 2)),
-            dma((4, 2)),
-            dma((4, 2)),
+            dma((8, 2, 2)),
+            dma((8, 2, 2)),
+            dma((8, 2)),
+            dma((8, 2)),
             dma((2, 2)),
             dma((2, 2)),
             dma((2, 2, 3)),
@@ -584,9 +611,11 @@
             dma((1,)),
             dma((3,)),
             dma((4,)),
-            dma((7,)),
-            dma((8,)),
-            dma((4,)),
+            dma((15,)),
+            dma((16,)),
+            dma((1,)),
+            dma((1,)),
+            dma((3,)),
             dma((4,)),
             pltpu.SemaphoreType.REGULAR,
             pltpu.SemaphoreType.REGULAR,

time: 55.1 us -> 53.7 us (0.975)
  the two profiles are of different devices: /device:TPU:32 before, /device:TPU:34 now
where the time goes in v3:
time: 53.7 us; the launch traced here: 53.5 us
  Pallas kernels  52.9 us (99%)
  between operations  0.64 us (1%)
    pallas_call x1, Pallas kernels, local(): pl.pallas_call(kernel, out_shape=out_shape, in_specs=[hbm] * 7, out_specs...  51.1 us
    pallas_call x1, Pallas kernels, local(): pl.pallas_call(move, out_shape=out_shape, in_specs=[hbm] * 3, out_specs=(...  1.8 us

profile of v3, /device:TPU:34, one launch (start us, length us, event | category | flops | bytes accessed | tf_op | source)
XLA Modules:
  0.0 53.5 jit_solution(1105175163018205535)
XLA Ops:
  0.6 51.1 %shard_map.94 = (f32[32,3072]{1,0:T(8,128)}, f32[1,4,128]{2,1,0:T(4,128)}, f32[8,2,32]{2,1,0:T(2,128)}) custom-call(s32[8]{0:T(128)} %feature_hbm.1, s32[8]{0:T(128)} %bin_hbm.1, s32[8]{0:T(128)} %missing_hbm.1, f32[32,3072]{1,0:T(8,128)} %bitcast.5, s32[1,3072]{1,0:T(1,128)} %bitcast.7, s32[1,3072]{1,0:T(1,128)} %bitcast.8, s32[32,3072]{1,0:T(8,128)} %bitcast.6), custom_call_target="tpu_custom_call" | custom-call | tf_op jit(solution)/shard_map/pallas_call | solution.py:566
  51.7 1.8 %shard_map.95 = (f32[32,3072]{1,0:T(8,128)}, f32[1,4,128]{2,1,0:T(4,128)}, f32[8,2,32]{2,1,0:T(2,128)}) custom-call(f32[32,3072]{1,0:T(8,128)} %get-tuple-element.9.new_ref, f32[1,4,128]{2,1,0:T(4,128)} %get-tuple-element.10.gain_ref, f32[8,2,32]{2,1,0:T(2,128)} %get-tuple-element.11.leaves_ref), custom_call_target="tpu_custom_call" | custom-call | tf_op jit(solution)/shard_map/pallas_call | solution.py:635

commit v4 on v3

--- a/solution.py
+++ b/solution.py
@@ -60,9 +60,13 @@
     hist,
     core_buf,
     y1_buf,
+    y1_late,
     y2_buf,
+    y2_late,
     z1_buf,
+    z1_late,
     direct_buf,
+    direct_late,
     flag_buf,
     far_flag,
     x_buf,
@@ -81,6 +85,8 @@
     z1_recv,
     direct_send,
     direct_recv,
+    late_send,
+    late_recv,
     flag_send,
     flag_recv,
     far_send,
@@ -279,15 +285,26 @@
     first_y = (ya, yb)
     second_y = (yb, ya)
 
+    def chunk_of(u):
+        return u // 2 if u < 4 else 2 + u % 2
+
+    def region(u, dest, first, count):
+        high = 2 * chunk_of(u) + 1
+        if u < 4:
+            return high, slice(None), pl.ds(2 * dest, 2), pl.ds(32 * (u % 2) + first // 2, count // 2)
+        return high, slice(None), 2 * dest + (u - 4) // 2, pl.ds(first, count)
+
     def part_of(u, dest, colour):
-        lines = pl.ds(32 * (u % 2) + 16 * colour, 16)
-        return hist.at[2 * (u // 2) + 1, :, pl.ds(2 * dest, 2), lines]
+        return region(u, dest, 32 * colour, 32)
+
+    def slots(u, early, late):
+        return early.at[u] if u < 4 else late.at[u - 4]
 
     def y1_copy(u, colour, part):
         dest = first_y[colour] if part else yc
         return remote(
-            part_of(u, dest, colour),
-            y1_buf.at[u, colour, part],
+            hist.at[part_of(u, dest, colour)],
+            slots(u, y1_buf, y1_late).at[colour, part],
             y1_send.at[u, colour, part],
             y1_recv.at[u, colour, part],
             at_y(first_y[colour]),
@@ -296,29 +313,40 @@
     def y2_copy(u, colour):
         dest = second_y[colour]
         return remote(
-            part_of(u, dest, colour),
-            y2_buf.at[u, colour],
+            hist.at[part_of(u, dest, colour)],
+            slots(u, y2_buf, y2_late).at[colour],
             y2_send.at[u, colour],
             y2_recv.at[u, colour],
             at_y(dest),
         )
 
-    def z1_copy(k, colour):
+    def z1_copy(u):
         return remote(
-            hist.at[2 * k + 1, :, pl.ds(2 * y, 2), pl.ds(32 * colour, 32)],
-            z1_buf.at[k // 2, colour],
-            z1_send.at[k // 2, colour],
-            z1_recv.at[k // 2, colour],
+            hist.at[region(u, y, 0, 64)],
+            slots(u, z1_buf, z1_late),
+            z1_send.at[u],
+            z1_recv.at[u],
             z_peer1,
         )
 
-    def direct_copy(k, colour, d):
+    def direct_copy(half, d):
         other = (quad + d) % 4
         return remote(
-            hist.at[2 * k + 1, other % 2, 2 * y + other // 2, pl.ds(32 * colour, 32)],
-            direct_buf.at[k // 2, colour, d - 1],
-            direct_send.at[k // 2, colour, d - 1],
-            direct_recv.at[k // 2, colour, d - 1],
+            hist.at[2 * z0 + 1, other % 2, 2 * y + other // 2, pl.ds(32 * half, 32)],
+            direct_buf.at[half, d - 1],
+            direct_send.at[half, d - 1],
+            direct_recv.at[half, d - 1],
+            at_z(other * 2 + z0),
+        )
+
+    def late_copy(nodes, high):
+        other = 2 * nodes + high
+        d = (other + 4 - quad) % 4
+        return d, remote(
+            hist.at[2 * (2 + z0) + 1, high, 2 * y + nodes],
+            direct_late.at[d],
+            late_send.at[nodes, high],
+            late_recv.at[d],
             at_z(other * 2 + z0),
         )
 
@@ -333,40 +361,42 @@
             for colour in range(2):
                 y1_copy(u, colour, part).start()
 
-    def add_lines(k, dest, first, count, incoming):
-        at = (2 * k + 1, slice(None), pl.ds(2 * dest, 2), slice(first, first + count))
+    def add(at, incoming):
         hist[at] = hist[at] + incoming
-
-    def add_part(u, dest, colour, incoming):
-        add_lines(u // 2, dest, 32 * (u % 2) + 16 * colour, 16, incoming)
 
     def after_y1(u):
         for colour in range(2):
             y1_copy(u, colour, 0).wait_recv()
-            add_part(u, second_y[colour], colour, y1_buf[u, colour, 0])
+            add(part_of(u, second_y[colour], colour), slots(u, y1_buf, y1_late)[colour, 0])
             y2_copy(u, colour).start()
         for colour in range(2):
             y1_copy(u, colour, 1).wait_recv()
-            add_part(u, y, colour, y1_buf[u, colour, 1])
+            add(part_of(u, y, colour), slots(u, y1_buf, y1_late)[colour, 1])
 
     def after_y2(u):
         for colour in range(2):
             y2_copy(u, colour).wait_recv()
-            add_part(u, y, colour, y2_buf[u, colour])
-
-        @pl.when(z0 != (u // 2) % 2)
-        def _():
-            z1_copy(u // 2, u % 2).start()
+            add(part_of(u, y, colour), slots(u, y2_buf, y2_late)[colour])
+
+        @pl.when(z0 != chunk_of(u) % 2)
+        def _():
+            z1_copy(u).start()
 
     def after_z1(u):
-        k, half = u // 2, u % 2
-
-        @pl.when(z0 == k % 2)
-        def _():
-            z1_copy(k, half).wait_recv()
-            add_lines(k, y, 32 * half, 32, z1_buf[k // 2, half])
-            for d in (2, 1, 3):
-                direct_copy(k, half, d).start()
+        @pl.when(z0 == chunk_of(u) % 2)
+        def _():
+            z1_copy(u).wait_recv()
+            add(region(u, y, 0, 64), slots(u, z1_buf, z1_late)[...])
+            if u < 4:
+                for d in (2, 1, 3):
+                    direct_copy(u % 2, d).start()
+            else:
+                for high in range(2):
+                    d, copy = late_copy((u - 4) // 2, high)
+
+                    @pl.when(d != 0)
+                    def _():
+                        copy.start()
 
     def step(s, carry):
         k = s // 2
@@ -493,15 +523,21 @@
     last = as_weights(same & (bin_in == BINS - 1))
     lane = lax.broadcasted_iota(jnp.int32, (1, 128), 1)
     for pair in range(2):
-        k = 2 * pair + z0
-        parts = []
-        for colour in range(2):
-            part = hist[2 * k + 1, z1, 2 * y + z2, 32 * colour : 32 * colour + 32]
-            for d in (2, 1, 3):
-                direct_copy(k, colour, d).wait_recv()
-                part = part + direct_buf[pair, colour, d - 1]
-            parts.append(part)
-        owned = jnp.concatenate(parts, axis=0)
+        if pair == 0:
+            parts = []
+            for half in range(2):
+                part = hist[2 * z0 + 1, z1, 2 * y + z2, 32 * half : 32 * half + 32]
+                for d in (1, 2, 3):
+                    direct_copy(half, d).wait_recv()
+                    part = part + direct_buf[half, d - 1]
+                parts.append(part)
+            owned = jnp.concatenate(parts, axis=0)
+        else:
+            owned = hist[2 * (2 + z0) + 1, z1, 2 * y + z2]
+            for d in (1, 2, 3):
+                slot = direct_late.at[d]
+                remote(slot, slot, late_send.at[0, 0], late_recv.at[d], z_peer2).wait_recv()
+                owned = owned + direct_late[d]
         left_base = exact_dot(owned, lower, NN)
         node_total = exact_dot(owned, every, NN)
         left_miss = left_base + exact_dot(owned, last, NN)
@@ -527,11 +563,23 @@
             y1_copy(u, colour, 0).wait_send()
             y1_copy(u, colour, 1).wait_send()
             y2_copy(u, colour).wait_send()
-    for pair in range(2):
-        for colour in range(2):
-            z1_copy(2 * pair + 1 - z0, colour).wait_send()
-            for d in (1, 2, 3):
-                direct_copy(2 * pair + z0, colour, d).wait_send()
+    for u in range(8):
+
+        @pl.when(z0 != chunk_of(u) % 2)
+        def _():
+            z1_copy(u).wait_send()
+
+    for half in range(2):
+        for d in (1, 2, 3):
+            direct_copy(half, d).wait_send()
+    for nodes in range(2):
+        for high in range(2):
+            d, copy = late_copy(nodes, high)
+
+            @pl.when(d != 0)
+            def _():
+                copy.wait_send()
+
     for store in stores:
         store.wait()
 
@@ -583,10 +631,14 @@
             pltpu.VMEM((256, rows), jnp.bfloat16),
             pltpu.VMEM((8, 2, 8, 64, 128), f32),
             pltpu.VMEM((4, 2, 8, 64, 128), f32),
-            pltpu.VMEM((8, 2, 2, 2, 2, 16, 128), f32),
-            pltpu.VMEM((8, 2, 2, 2, 16, 128), f32),
-            pltpu.VMEM((2, 2, 2, 2, 32, 128), f32),
-            pltpu.VMEM((2, 2, 3, 32, 128), f32),
+            pltpu.VMEM((4, 2, 2, 2, 2, 16, 128), f32),
+            pltpu.VMEM((4, 2, 2, 2, 32, 128), f32),
+            pltpu.VMEM((4, 2, 2, 2, 16, 128), f32),
+            pltpu.VMEM((4, 2, 2, 32, 128), f32),
+            pltpu.VMEM((4, 2, 2, 32, 128), f32),
+            pltpu.VMEM((4, 2, 64, 128), f32),
+            pltpu.VMEM((2, 3, 32, 128), f32),
+            pltpu.VMEM((4, 64, 128), f32),
             pltpu.VMEM((4, 1, rows), f32),
             pltpu.VMEM((2, 1, rows), f32),
             pltpu.VMEM((4, 8, 128), f32),
@@ -601,10 +653,12 @@
             dma((8, 2, 2)),
             dma((8, 2)),
             dma((8, 2)),
+            dma((8,)),
+            dma((8,)),
+            dma((2, 3)),
+            dma((2, 3)),
             dma((2, 2)),
-            dma((2, 2)),
-            dma((2, 2, 3)),
-            dma((2, 2, 3)),
+            dma((4,)),
             dma((3,)),
             dma((4,)),
             dma((1,)),

time: 53.7 us -> 50.9 us (0.948)
  the two profiles are of different devices: /device:TPU:34 before, /device:TPU:38 now
where the time goes in v4:
time: 50.9 us; the launch traced here: 50.7 us
  Pallas kernels  50.1 us (98%)
  between operations  0.64 us (1%)
    pallas_call x1, Pallas kernels, local(): pl.pallas_call(kernel, out_shape=out_shape, in_specs=[hbm] * 7, out_specs...  48.3 us
    pallas_call x1, Pallas kernels, local(): pl.pallas_call(move, out_shape=out_shape, in_specs=[hbm] * 3, out_specs=(...  1.8 us

profile of v4, /device:TPU:38, one launch (start us, length us, event | category | flops | bytes accessed | tf_op | source)
XLA Modules:
  0.0 50.7 jit_solution(12019895742709464910)
XLA Ops:
  0.6 48.3 %shard_map.94 = (f32[32,3072]{1,0:T(8,128)}, f32[1,4,128]{2,1,0:T(4,128)}, f32[8,2,32]{2,1,0:T(2,128)}) custom-call(s32[8]{0:T(128)} %feature_hbm.1, s32[8]{0:T(128)} %bin_hbm.1, s32[8]{0:T(128)} %missing_hbm.1, f32[32,3072]{1,0:T(8,128)} %bitcast.5, s32[1,3072]{1,0:T(1,128)} %bitcast.7, s32[1,3072]{1,0:T(1,128)} %bitcast.8, s32[32,3072]{1,0:T(8,128)} %bitcast.6), custom_call_target="tpu_custom_call" | custom-call | tf_op jit(solution)/shard_map/pallas_call | solution.py:614
  48.9 1.8 %shard_map.95 = (f32[32,3072]{1,0:T(8,128)}, f32[1,4,128]{2,1,0:T(4,128)}, f32[8,2,32]{2,1,0:T(2,128)}) custom-call(f32[32,3072]{1,0:T(8,128)} %get-tuple-element.9.new_ref, f32[1,4,128]{2,1,0:T(4,128)} %get-tuple-element.10.gain_ref, f32[8,2,32]{2,1,0:T(2,128)} %get-tuple-element.11.leaves_ref), custom_call_target="tpu_custom_call" | custom-call | tf_op jit(solution)/shard_map/pallas_call | solution.py:689

commit v5 on v3

--- a/solution.py
+++ b/solution.py
@@ -279,15 +279,23 @@
     first_y = (ya, yb)
     second_y = (yb, ya)
 
+    chunks = (0, 0, 1, 2, 3, 1, 2, 3)
+    parities = (0, 1, 0, 0, 0, 1, 1, 1)
+
+    def chunk_of(u):
+        return chunks[u]
+
+    def region(u, dest, first, count):
+        return 2 * chunks[u] + 1, slice(None), 2 * dest + parities[u], pl.ds(first, count)
+
     def part_of(u, dest, colour):
-        lines = pl.ds(32 * (u % 2) + 16 * colour, 16)
-        return hist.at[2 * (u // 2) + 1, :, pl.ds(2 * dest, 2), lines]
+        return region(u, dest, 32 * colour, 32)
 
     def y1_copy(u, colour, part):
         dest = first_y[colour] if part else yc
         return remote(
-            part_of(u, dest, colour),
-            y1_buf.at[u, colour, part],
+            hist.at[part_of(u, dest, colour)],
+            y1_buf.at[u].at[colour, part],
             y1_send.at[u, colour, part],
             y1_recv.at[u, colour, part],
             at_y(first_y[colour]),
@@ -296,29 +304,30 @@
     def y2_copy(u, colour):
         dest = second_y[colour]
         return remote(
-            part_of(u, dest, colour),
-            y2_buf.at[u, colour],
+            hist.at[part_of(u, dest, colour)],
+            y2_buf.at[u].at[colour],
             y2_send.at[u, colour],
             y2_recv.at[u, colour],
             at_y(dest),
         )
 
-    def z1_copy(k, colour):
+    def z1_copy(u):
         return remote(
-            hist.at[2 * k + 1, :, pl.ds(2 * y, 2), pl.ds(32 * colour, 32)],
-            z1_buf.at[k // 2, colour],
-            z1_send.at[k // 2, colour],
-            z1_recv.at[k // 2, colour],
+            hist.at[region(u, y, 0, 64)],
+            z1_buf.at[u],
+            z1_send.at[u],
+            z1_recv.at[u],
             z_peer1,
         )
 
-    def direct_copy(k, colour, d):
-        other = (quad + d) % 4
-        return remote(
-            hist.at[2 * k + 1, other % 2, 2 * y + other // 2, pl.ds(32 * colour, 32)],
-            direct_buf.at[k // 2, colour, d - 1],
-            direct_send.at[k // 2, colour, d - 1],
-            direct_recv.at[k // 2, colour, d - 1],
+    def direct_copy(pair, nodes, high):
+        other = 2 * nodes + high
+        d = (other + 4 - quad) % 4
+        return d, remote(
+            hist.at[4 * pair + 2 * z0 + 1, high, 2 * y + nodes],
+            direct_buf.at[pair, d],
+            direct_send.at[pair, nodes, high],
+            direct_recv.at[pair, d],
             at_z(other * 2 + z0),
         )
 
@@ -333,40 +342,39 @@
             for colour in range(2):
                 y1_copy(u, colour, part).start()
 
-    def add_lines(k, dest, first, count, incoming):
-        at = (2 * k + 1, slice(None), pl.ds(2 * dest, 2), slice(first, first + count))
+    def add(at, incoming):
         hist[at] = hist[at] + incoming
-
-    def add_part(u, dest, colour, incoming):
-        add_lines(u // 2, dest, 32 * (u % 2) + 16 * colour, 16, incoming)
 
     def after_y1(u):
         for colour in range(2):
             y1_copy(u, colour, 0).wait_recv()
-            add_part(u, second_y[colour], colour, y1_buf[u, colour, 0])
+            add(part_of(u, second_y[colour], colour), y1_buf[u, colour, 0])
             y2_copy(u, colour).start()
+
+    def after_y2(u):
         for colour in range(2):
             y1_copy(u, colour, 1).wait_recv()
-            add_part(u, y, colour, y1_buf[u, colour, 1])
-
-    def after_y2(u):
-        for colour in range(2):
             y2_copy(u, colour).wait_recv()
-            add_part(u, y, colour, y2_buf[u, colour])
-
-        @pl.when(z0 != (u // 2) % 2)
-        def _():
-            z1_copy(u // 2, u % 2).start()
+            add(
+                part_of(u, y, colour),
+                y1_buf[u, colour, 1] + y2_buf[u, colour],
+            )
+
+        @pl.when(z0 != chunk_of(u) % 2)
+        def _():
+            z1_copy(u).start()
 
     def after_z1(u):
-        k, half = u // 2, u % 2
-
-        @pl.when(z0 == k % 2)
-        def _():
-            z1_copy(k, half).wait_recv()
-            add_lines(k, y, 32 * half, 32, z1_buf[k // 2, half])
-            for d in (2, 1, 3):
-                direct_copy(k, half, d).start()
+        @pl.when(z0 == chunk_of(u) % 2)
+        def _():
+            z1_copy(u).wait_recv()
+            add(region(u, y, 0, 64), z1_buf[u])
+            for high in range(2):
+                d, copy = direct_copy(chunks[u] // 2, parities[u], high)
+
+                @pl.when(d != 0)
+                def _():
+                    copy.start()
 
     def step(s, carry):
         k = s // 2
@@ -422,12 +430,11 @@
         @pl.when(s == 5)
         def _():
             after_y1(0)
+
+        @pl.when(s == 6)
+        def _():
             send_y1(3)
-
-        @pl.when(s == 6)
-        def _():
             after_y1(1)
-            send_y1(4)
 
         @pl.when(s == 7)
         def _():
@@ -437,10 +444,10 @@
 
     lax.fori_loop(0, 8, step, 0)
 
+    after_core(3)
+    send_y1(4)
     for u in range(2, 8):
         after_y1(u)
-        if u == 2:
-            after_core(3)
         if u + 3 < 8:
             send_y1(u + 3)
         after_y2(u - 2)
@@ -493,15 +500,11 @@
     last = as_weights(same & (bin_in == BINS - 1))
     lane = lax.broadcasted_iota(jnp.int32, (1, 128), 1)
     for pair in range(2):
-        k = 2 * pair + z0
-        parts = []
-        for colour in range(2):
-            part = hist[2 * k + 1, z1, 2 * y + z2, 32 * colour : 32 * colour + 32]
-            for d in (2, 1, 3):
-                direct_copy(k, colour, d).wait_recv()
-                part = part + direct_buf[pair, colour, d - 1]
-            parts.append(part)
-        owned = jnp.concatenate(parts, axis=0)
+        owned = hist[4 * pair + 2 * z0 + 1, z1, 2 * y + z2]
+        for d in (1, 2, 3):
+            slot = direct_buf.at[pair, d]
+            remote(slot, slot, direct_send.at[0, 0, 0], direct_recv.at[pair, d], z_peer2).wait_recv()
+            owned = owned + direct_buf[pair, d]
         left_base = exact_dot(owned, lower, NN)
         node_total = exact_dot(owned, every, NN)
         left_miss = left_base + exact_dot(owned, last, NN)
@@ -527,11 +530,21 @@
             y1_copy(u, colour, 0).wait_send()
             y1_copy(u, colour, 1).wait_send()
             y2_copy(u, colour).wait_send()
+    for u in range(8):
+
+        @pl.when(z0 != chunk_of(u) % 2)
+        def _():
+            z1_copy(u).wait_send()
+
     for pair in range(2):
-        for colour in range(2):
-            z1_copy(2 * pair + 1 - z0, colour).wait_send()
-            for d in (1, 2, 3):
-                direct_copy(2 * pair + z0, colour, d).wait_send()
+        for nodes in range(2):
+            for high in range(2):
+                d, copy = direct_copy(pair, nodes, high)
+
+                @pl.when(d != 0)
+                def _():
+                    copy.wait_send()
+
     for store in stores:
         store.wait()
 
@@ -583,10 +596,10 @@
             pltpu.VMEM((256, rows), jnp.bfloat16),
             pltpu.VMEM((8, 2, 8, 64, 128), f32),
             pltpu.VMEM((4, 2, 8, 64, 128), f32),
-            pltpu.VMEM((8, 2, 2, 2, 2, 16, 128), f32),
-            pltpu.VMEM((8, 2, 2, 2, 16, 128), f32),
-            pltpu.VMEM((2, 2, 2, 2, 32, 128), f32),
-            pltpu.VMEM((2, 2, 3, 32, 128), f32),
+            pltpu.VMEM((8, 2, 2, 2, 32, 128), f32),
+            pltpu.VMEM((8, 2, 2, 32, 128), f32),
+            pltpu.VMEM((8, 2, 64, 128), f32),
+            pltpu.VMEM((2, 4, 64, 128), f32),
             pltpu.VMEM((4, 1, rows), f32),
             pltpu.VMEM((2, 1, rows), f32),
             pltpu.VMEM((4, 8, 128), f32),
@@ -601,10 +614,10 @@
             dma((8, 2, 2)),
             dma((8, 2)),
             dma((8, 2)),
-            dma((2, 2)),
-            dma((2, 2)),
-            dma((2, 2, 3)),
-            dma((2, 2, 3)),
+            dma((8,)),
+            dma((8,)),
+            dma((2, 2, 2)),
+            dma((2, 4)),
             dma((3,)),
             dma((4,)),
             dma((1,)),

time: 53.7 us -> 50.2 us (0.935)
  the two profiles are of different devices: /device:TPU:34 before, /device:TPU:32 now
where the time goes in v5:
time: 50.2 us; the launch traced here: 50.1 us
  Pallas kernels  49.4 us (98%)
  between operations  0.64 us (1%)
    pallas_call x1, Pallas kernels, local(): pl.pallas_call(kernel, out_shape=out_shape, in_specs=[hbm] * 7, out_specs...  47.6 us
    pallas_call x1, Pallas kernels, local(): pl.pallas_call(move, out_shape=out_shape, in_specs=[hbm] * 3, out_specs=(...  1.8 us

profile of v5, /device:TPU:32, one launch (start us, length us, event | category | flops | bytes accessed | tf_op | source)
XLA Modules:
  0.0 50.1 jit_solution(1636913590442570511)
XLA Ops:
  0.6 47.6 %shard_map.94 = (f32[32,3072]{1,0:T(8,128)}, f32[1,4,128]{2,1,0:T(4,128)}, f32[8,2,32]{2,1,0:T(2,128)}) custom-call(s32[8]{0:T(128)} %feature_hbm.1, s32[8]{0:T(128)} %bin_hbm.1, s32[8]{0:T(128)} %missing_hbm.1, f32[32,3072]{1,0:T(8,128)} %bitcast.5, s32[1,3072]{1,0:T(1,128)} %bitcast.7, s32[1,3072]{1,0:T(1,128)} %bitcast.8, s32[32,3072]{1,0:T(8,128)} %bitcast.6), custom_call_target="tpu_custom_call" | custom-call | tf_op jit(solution)/shard_map/pallas_call | solution.py:579
  48.3 1.8 %shard_map.95 = (f32[32,3072]{1,0:T(8,128)}, f32[1,4,128]{2,1,0:T(4,128)}, f32[8,2,32]{2,1,0:T(2,128)}) custom-call(f32[32,3072]{1,0:T(8,128)} %get-tuple-element.9.new_ref, f32[1,4,128]{2,1,0:T(4,128)} %get-tuple-element.10.gain_ref, f32[8,2,32]{2,1,0:T(2,128)} %get-tuple-element.11.leaves_ref), custom_call_target="tpu_custom_call" | custom-call | tf_op jit(solution)/shard_map/pallas_call | solution.py:648

commit v6 on v5

--- a/solution.py
+++ b/solution.py
@@ -450,6 +450,8 @@
         after_y1(u)
         if u + 3 < 8:
             send_y1(u + 3)
+        if u >= 4:
+            after_z1(u - 4)
         after_y2(u - 2)
         if u == 2:
             pl.semaphore_wait(vouch4, 2)
@@ -459,8 +461,6 @@
             far_copy.start()
         if u == 3:
             after_pair()
-        if u >= 4:
-            after_z1(u - 4)
     after_y2(6)
     after_z1(4)
     after_y2(7)

time: 50.2 us -> 49.9 us (level)
    pallas_call x1, Pallas kernels: 47.6 us -> 47.1 us  [local(): pl.pallas_call(kernel, out_shape=out_shape, in_specs=[hbm] * 7, out_specs...]
where the time goes in v6:
time: 49.9 us; the launch traced here: 49.6 us
  Pallas kernels  48.9 us (98%)
  between operations  0.64 us (1%)
    pallas_call x1, Pallas kernels, local(): pl.pallas_call(kernel, out_shape=out_shape, in_specs=[hbm] * 7, out_specs...  47.1 us
    pallas_call x1, Pallas kernels, local(): pl.pallas_call(move, out_shape=out_shape, in_specs=[hbm] * 3, out_specs=(...  1.8 us

profile of v6, /device:TPU:32, one launch (start us, length us, event | category | flops | bytes accessed | tf_op | source)
XLA Modules:
  0.0 49.6 jit_solution(4368272148959240240)
XLA Ops:
  0.6 47.1 %shard_map.94 = (f32[32,3072]{1,0:T(8,128)}, f32[1,4,128]{2,1,0:T(4,128)}, f32[8,2,32]{2,1,0:T(2,128)}) custom-call(s32[8]{0:T(128)} %feature_hbm.1, s32[8]{0:T(128)} %bin_hbm.1, s32[8]{0:T(128)} %missing_hbm.1, f32[32,3072]{1,0:T(8,128)} %bitcast.5, s32[1,3072]{1,0:T(1,128)} %bitcast.7, s32[1,3072]{1,0:T(1,128)} %bitcast.8, s32[32,3072]{1,0:T(8,128)} %bitcast.6), custom_call_target="tpu_custom_call" | custom-call | tf_op jit(solution)/shard_map/pallas_call | solution.py:579
  47.8 1.8 %shard_map.95 = (f32[32,3072]{1,0:T(8,128)}, f32[1,4,128]{2,1,0:T(4,128)}, f32[8,2,32]{2,1,0:T(2,128)}) custom-call(f32[32,3072]{1,0:T(8,128)} %get-tuple-element.9.new_ref, f32[1,4,128]{2,1,0:T(4,128)} %get-tuple-element.10.gain_ref, f32[8,2,32]{2,1,0:T(2,128)} %get-tuple-element.11.leaves_ref), custom_call_target="tpu_custom_call" | custom-call | tf_op jit(solution)/shard_map/pallas_call | solution.py:648
